TPU v7x, 32 devices: a whole 2x2x4 slice. The times are simulated.
32 devices in a mesh: dp: 2 (over x), expert: 16 (over z, y, core).
Axes of the slice: x: 2, y: 2, z: 4, core: 2. Of those that a mesh axis runs over, the one named last changes fastest.
Arguments:
- expert_out: bfloat16 [2, 128, 16, 2, 7168], P('dp', 'expert'), may hold values from -6 to 6
- expert_ids: int32 [256, 8], P(('dp', 'expert')), may hold values from 0 to 127, all different within a row; in each aligned block of 8 rows (0 to 7, 8 to 15, ...) at most 2 rows name the same one
- gate_weight: float32 [256, 8], P(('dp', 'expert')), may hold values from 0.05 to 1
Outputs:
- combined: bfloat16 [256, 7168], P(('dp', 'expert'))
- expert_counts: int32 [128], P('expert')
- expert_rms: float32 [128], P('expert')
Inputs may be any that keep to these rules, and one draw needn't show every extreme that they name: `expert_ids`: in each aligned block of 8 tokens no expert is named by more than 2 rows, and a token names 8 different experts; every expert is named by some token.
All inputs are finite; a program needn't handle non-finite values.
Results may differ from a plain program's by a relative error of at most 0.008.
Values may be sent and summed in bfloat16 or wider, within the bound.
No kernel may reach another device: no remote copies, remote signals or barrier semaphores. Data moves between devices by JAX's collectives and lax.ppermute only.
A program may use at most 64 MiB of HBM per device.

v0:
```python
import jax
import jax.numpy as jnp
from jax import lax
from jax.sharding import PartitionSpec as P

EXPERTS = 128
TOP = 8
CAP = 2


epsilon = 1e-06


def slot_index_of(block_ids):
    flat = block_ids.reshape(-1)
    total_rows = flat.shape[0]
    one_hot = (flat[:, None] == jnp.arange(EXPERTS, dtype=jnp.int32)[None, :]).astype(jnp.float32)
    earlier = (
        jnp.arange(total_rows, dtype=jnp.int32)[:, None]
        > jnp.arange(total_rows, dtype=jnp.int32)[None, :]
    ).astype(jnp.float32)
    before = jnp.dot(earlier, one_hot, precision=lax.Precision.HIGHEST)
    position = jnp.sum(before * one_hot, axis=1).astype(jnp.int32)
    return flat * CAP + position


def holder_combine(picked, ids, gates, per_holder):
    holder = ids // per_holder
    same = (holder[:, :, None] == holder[:, None, :]).astype(jnp.float32)
    weights = same * gates[:, None, :]
    partial_value = jnp.einsum(
        "tkj,tjd->tkd", weights, picked.astype(jnp.float32), precision=lax.Precision.HIGHEST
    )
    partial_value = partial_value.astype(jnp.bfloat16).astype(jnp.float32)
    lower = (
        jnp.arange(TOP, dtype=jnp.int32)[:, None] > jnp.arange(TOP, dtype=jnp.int32)[None, :]
    ).astype(jnp.float32)
    repeats = jnp.sum(same * lower[None, :, :], axis=2)
    leading = (repeats < 0.5).astype(jnp.float32)
    return jnp.sum(leading[:, :, None] * partial_value, axis=1).astype(jnp.bfloat16)


def body(expert_out, expert_ids, gate_weight):
    tok_rows = expert_ids.shape[0]
    width = expert_out.shape[4]
    local_experts = expert_out.shape[1]
    slot_index = slot_index_of(expert_ids)
    arrived = lax.all_to_all(expert_out, "expert", split_axis=2, concat_axis=1, tiled=True)
    received = arrived.reshape(EXPERTS * CAP, width)
    picked = jnp.take(received, slot_index, axis=0).reshape(tok_rows, TOP, width)
    combined = holder_combine(picked, expert_ids, gate_weight, local_experts)
    occupied = jnp.sum(
        (slot_index[:, None] == jnp.arange(EXPERTS * CAP, dtype=jnp.int32)[None, :]).astype(
            jnp.float32
        ),
        axis=0,
    )
    local_squares = jnp.sum(jnp.square(expert_out.astype(jnp.float32)), axis=4)
    moved_squares = lax.all_to_all(
        local_squares, "expert", split_axis=2, concat_axis=1, tiled=True
    ).reshape(EXPERTS * CAP)
    sum_part = jnp.sum((occupied * moved_squares).reshape(EXPERTS, CAP), axis=1)
    count_part = jnp.sum(occupied.reshape(EXPERTS, CAP), axis=1)
    total_squares, total_counts = lax.psum((sum_part, count_part), ("dp", "expert"))
    start = lax.axis_index("expert") * local_experts
    total_squares = lax.dynamic_slice_in_dim(total_squares, start, local_experts, 0)
    total_counts = lax.dynamic_slice_in_dim(total_counts, start, local_experts, 0)
    expert_rms = jnp.sqrt(total_squares / (total_counts * width) + epsilon)
    return (combined, total_counts.astype(jnp.int32), expert_rms)


def solution(mesh):
    return jax.shard_map(
        body,
        mesh=mesh,
        in_specs=(
            P("dp", "expert", None, None, None),
            P(("dp", "expert"), None),
            P(("dp", "expert"), None),
        ),
        out_specs=(P(("dp", "expert"), None), P("expert"), P("expert")),
        check_vma=False,
    )
```

profile of v0, /device:TPU:0, one launch (start us, length us, event | category | flops | bytes accessed | tf_op | source)
XLA Modules:
  0.0 146.6 jit_solution(2664625623642666765)
XLA Ops:
  0.6 5.9 %multiply_reduce_fusion = f32[8,16,2]{2,1,0:T(8,128)S(1)} fusion(bf16[1,8,16,2,7168]{4,3,2,1,0:T(2,128)(2,1)} %param.3), kind=kLoop, calls=%fused_computation.4 | loop fusion | flops 5504768 | bytes 3671040 | tf_op jit(solution)/shard_map/reduce_sum | solution.py:58
  6.5 0.8 copy.12
  7.3 7.4 %all-to-all-start.1 = ((f32[1,8,16,2]{1,3,0,2:T(2,128)}), f32[1,8,16,2]{1,3,0,2:T(2,128)S(1)}, u32[]{:S(2)}, u32[]{:S(2)}) async-start(f32[1,8,16,2]{1,3,0,2:T(2,128)} %copy.12), calls=%async_computation.1 | async-start | bytes 32768 | tf_op jit(solution)/shard_map/all_to_all | solution.py:59
  14.7 7.3 %copy.11 = bf16[1,8,16,2,7168]{4,3,1,0,2:T(2,128)(2,1)} copy(bf16[1,8,16,2,7168]{4,3,2,1,0:T(2,128)(2,1)} %param.3) | data formatting | bytes 7340032 | tf_op args[0]
  22.0 0.0 copy-start
  22.0 0.0 all-to-all-done.1
  22.0 6.2 %all-to-all-start = ((bf16[1,8,16,2,7168]{4,3,1,0,2:T(2,128)(2,1)}), bf16[1,8,16,2,7168]{4,3,1,0,2:T(2,128)(2,1)}, u32[]{:S(2)}, u32[]{:S(2)}) async-start(bf16[1,8,16,2,7168]{4,3,1,0,2:T(2,128)(2,1)} %copy.11), calls=%async_computation | async-start | bytes 7340032 | tf_op jit(solution)/shard_map/all_to_all | solution.py:48
  28.2 0.0 copy-done
  28.2 0.1 reshape.97
  28.3 0.1 mul.71
  28.4 0.3 fusion.3
  28.7 0.1 convert_element_type.61
  28.8 0.1 convert_reduce_fusion
  28.9 0.1 reshape.99
  29.1 0.2 fusion.7
  29.2 0.2 copy.13
  29.4 0.1 fusion.6
  29.5 101.6 %all-reduce = (f32[128]{0:T(128)S(1)}, f32[128]{0:T(128)S(1)}) all-reduce(f32[128]{0:T(128)S(1)} %get-tuple-element.4, f32[128]{0:T(128)S(1)} %get-tuple-element.3), channel_id=1, replica_groups=mesh['dp'=2,'expert'=16] {'dp','expert'}, use_global_device_ids=true, to_apply=%region_5.6 | all-reduce | flops 256 | bytes 2048 | tf_op jit(solution)/shard_map/psum | solution.py:64
  131.1 0.6 add_sqrt_fusion
  131.7 0.0 all-to-all-done
  131.7 8.4 %reshape.98 = bf16[256,7168]{1,0:T(8,128)(2,1)} reshape(bf16[1,16,8,1,2,7168]{5,4,2,1,3,0:T(2,128)(2,1)} %bitcast.1) | data formatting | bytes 7340032 | tf_op jit(solution)/shard_map/reshape | solution.py:49
  140.1 4.5 %gather_fusion = bf16[64,7168]{1,0:T(8,128)(2,1)S(1)} fusion(bf16[256,7168]{1,0:T(8,128)(2,1)} %reshape.98, s32[1024]{0:T(1024)S(1)} %pad_clamp_fusion), kind=kCustom, calls=%fused_computation | custom fusion | bytes 1835264 | tf_op jit(solution)/shard_map/jit(_take)/gather | solution.py:50
  144.6 0.0 copy-done.1
  144.6 2.0 %fusion.2 = bf16[8,7168]{1,0:T(8,128)(2,1)} fusion(bf16[64,7168]{1,0:T(8,128)(2,1)S(1)} %gather_fusion, f32[8,8]{1,0:T(8,128)S(1)} %get-tuple-element.12, pred[8,8]{1,0:T(8,128)(4,1)S(1)} %get-tuple-element.11, f32[8,8]{1,0:T(8,128)S(1)} %copy-done.1, s32[8,8]{1,0:T(8,128)S(1)} %get-tuple-element.7), kind=kOutput, calls=%fused_computation.5 | convolution fusion | flops 46277632 | bytes 1033024 | tf_op jit(solution)/shard_map/tkj,tjd->tkd/dot_general | solution.py:31
  (8 shorter events, 0.1 us)
Async XLA Ops:
  7.3 14.7 %all-to-all-start.1 = ((f32[1,8,16,2]{1,3,0,2:T(2,128)}), f32[1,8,16,2]{1,3,0,2:T(2,128)S(1)}, u32[]{:S(2)}, u32[]{:S(2)}) async-start(f32[1,8,16,2]{1,3,0,2:T(2,128)} %copy.12), calls=%async_computation.1 | async-start | bytes 32768 | tf_op jit(solution)/shard_map/all_to_all | solution.py:59
  22.0 6.2 %copy-start = (s32[8,8]{1,0:T(8,128)S(1)}, s32[8,8]{1,0:T(8,128)}, u32[]{:S(2)}) copy-start(s32[8,8]{1,0:T(8,128)} %param.4) | copy-start | bytes 772
  22.0 109.7 %all-to-all-start = ((bf16[1,8,16,2,7168]{4,3,1,0,2:T(2,128)(2,1)}), bf16[1,8,16,2,7168]{4,3,1,0,2:T(2,128)(2,1)}, u32[]{:S(2)}, u32[]{:S(2)}) async-start(bf16[1,8,16,2,7168]{4,3,1,0,2:T(2,128)(2,1)} %copy.11), calls=%async_computation | async-start | bytes 7340032 | tf_op jit(solution)/shard_map/all_to_all | solution.py:48
  140.1 4.5 %copy-start.1 = (f32[8,8]{1,0:T(8,128)S(1)}, f32[8,8]{1,0:T(8,128)}, u32[]{:S(2)}) copy-start(f32[8,8]{1,0:T(8,128)} %param.5) | copy-start | bytes 772
where the time goes:
time: 147 us
  blocking collectives  102 us (69%)
  local copies, waits for them, and re-layouts  21.5 us (15%)
  starting transfers between devices  13.6 us (9%)
  other arithmetic  6.91 us (5%)
  matrix products  2.32 us (2%)
    psum x1, blocking collectives, body(): lax.psum((sum_part, count_part), ('dp', 'expert'))  102 us
    reshape x1, local copies, waits for them, and re-layouts, body(): received = arrived.reshape(EXPERTS * CAP, width)  8.4 us
    all_to_all x1, starting transfers between devices, body(): lax.all_to_all(local_squares, 'expert', split_axis=2, concat_axis=1, tile...  7.41 us
    unnamed x5, local copies, waits for them, and re-layouts  7.26 us
    all_to_all x1, starting transfers between devices, body(): lax.all_to_all(expert_out, 'expert', split_axis=2, concat_axis=1, tiled=T...  6.18 us
    reduce_sum x1, other arithmetic, body(): local_squares = jnp.sum(jnp.square(expert_out.astype(jnp.float32)), axis=4)  5.9 us
    gather x1, local copies, waits for them, and re-layouts, body(): jnp.take(received, slot_index, axis=0).reshape(tok_rows, TOP, width)  4.48 us
  transfers between devices with their start and end apart: 2, of which 0 were waited for; matrix products, arithmetic and copies ran while one was open for 6% of the time, Pallas kernels for 0%

commit v1 on v0

v1 whole, which is shorter than its diff:
```python
import functools

import jax
import jax.numpy as jnp
from jax import lax
from jax.experimental import pallas as pl
from jax.experimental.pallas import tpu as pltpu
from jax.sharding import PartitionSpec as P

LANES = 128
GROUP = 8

epsilon = 1e-06


def weights_of(block, lane_expert, lane_slot, top):
    tokens = block.shape[0]
    shape = (tokens, lane_expert.shape[1])
    named = jnp.zeros(shape, jnp.float32)
    gate = jnp.zeros(shape, jnp.float32)
    for k in range(top):
        same = jnp.broadcast_to(block[:, k : k + 1], shape) == lane_expert
        named = named + jnp.where(same, 1.0, 0.0)
        gate = gate + jnp.where(same, jnp.broadcast_to(block[:, top + k : top + k + 1], shape), 0.0)
    row = lax.broadcasted_iota(jnp.int32, shape, 0)
    earlier = named
    shift = 1
    while shift < tokens:
        earlier = earlier + jnp.where(row >= shift, pltpu.roll(earlier, shift, 0), 0.0)
        shift *= 2
    earlier = earlier - named
    return jnp.where(earlier == lane_slot, gate, 0.0)


def combine_kernel(me_ref, gates_ref, own_hbm, other_hbm, out_ref, buffer, sems, *, sources, first, last, top, cap):
    me = me_ref[0]
    experts, tokens = own_hbm.shape[0], gates_ref.shape[1]
    rows = GROUP * cap
    span = pl.ds(first * rows, (last - first) * rows)

    def copies(i):
        source = ((me >> 1) ^ sources(i)) * 2 + (me & 1)
        return source, [
            pltpu.make_async_copy(ref.at[:, source, span, :], buffer.at[i, h], sems.at[i, h])
            for h, ref in enumerate((own_hbm, other_hbm))
        ]

    @pl.loop(0, out_ref.shape[0])
    def _(i):
        for copy in copies(i)[1]:
            copy.start()

    depth = 2 * experts * rows
    lane = lax.broadcasted_iota(jnp.int32, (tokens, depth), 1)
    local = (lane // rows) % experts
    holder = jnp.where(lane < experts * rows, me, me ^ 1)
    lane_expert = (holder * experts + local).astype(jnp.float32)
    lane_slot = (lane % cap).astype(jnp.float32)
    wide = lax.broadcasted_iota(jnp.int32, (GROUP, tokens, depth), 2)
    same_tile = (wide // cap) % GROUP == lax.broadcasted_iota(jnp.int32, wide.shape, 0)

    @pl.loop(0, out_ref.shape[0])
    def _(i):
        source, waits = copies(i)
        weights = weights_of(gates_ref[source], lane_expert, lane_slot, top)
        weights = jnp.where(same_tile, jnp.broadcast_to(weights[None], wide.shape), 0.0)
        weights = weights.reshape(GROUP * tokens, depth)
        high = weights.astype(jnp.bfloat16)
        low = (weights - high.astype(jnp.float32)).astype(jnp.bfloat16)
        both = jnp.concatenate([high, low], axis=0)
        for copy in waits:
            copy.wait()
        for b in range(last - first):
            part = buffer[i, :, :, b * rows : (b + 1) * rows, :].reshape(depth, LANES)
            total = jnp.dot(both, part, preferred_element_type=jnp.float32)
            total = total[: GROUP * tokens] + total[GROUP * tokens :]
            out_ref[i, b * GROUP * tokens : (b + 1) * GROUP * tokens, :] = total.astype(out_ref.dtype)


def combine(me, gates, own, other, sources, count, first, last, top, cap):
    experts = own.shape[0]
    tokens = gates.shape[1]
    rows = (last - first) * GROUP
    kernel = functools.partial(
        combine_kernel, sources=sources, first=first, last=last, top=top, cap=cap
    )
    return pl.pallas_call(
        kernel,
        out_shape=jax.ShapeDtypeStruct((count, rows * tokens, LANES), jnp.bfloat16),
        in_specs=[
            pl.BlockSpec(memory_space=pltpu.SMEM),
            pl.BlockSpec(memory_space=pltpu.VMEM),
            pl.BlockSpec(memory_space=pl.ANY),
            pl.BlockSpec(memory_space=pl.ANY),
        ],
        out_specs=pl.BlockSpec(memory_space=pltpu.VMEM),
        scratch_shapes=[
            pltpu.VMEM((count, 2, experts, rows * cap, LANES), jnp.bfloat16),
            pltpu.SemaphoreType.DMA((count, 2)),
        ],
        name="combine",
    )(me, gates, own, other)


def statistics_kernel(me_ref, gates_ref, own_ref, sums_ref, counts_ref, *, top, cap):
    step = pl.program_id(0)
    experts, height = own_ref.shape[0], own_ref.shape[2]
    tokens = gates_ref.shape[1]
    rows = GROUP * cap
    depth = experts * rows

    @pl.when(step == 0)
    def _():
        sums_ref[...] = jnp.zeros_like(sums_ref)
        counts_ref[...] = jnp.zeros_like(counts_ref)

    lane = lax.broadcasted_iota(jnp.int32, (tokens, depth), 1)
    lane_expert = (me_ref[0] * experts + lane // rows).astype(jnp.float32)
    block = gates_ref[0]
    named = jnp.zeros((tokens, depth), jnp.float32)
    for k in range(top):
        named = named + jnp.where(jnp.broadcast_to(block[:, k : k + 1], named.shape) == lane_expert, 1.0, 0.0)
    times = jnp.sum(named, axis=0, keepdims=True)
    shape = (experts, depth)
    lane = lax.broadcasted_iota(jnp.int32, shape, 1)
    mine = lane // rows == lax.broadcasted_iota(jnp.int32, shape, 0)
    used = jnp.where(
        mine & (jnp.broadcast_to(times, shape) > (lane % cap).astype(jnp.float32)), 1.0, 0.0
    )
    counts_ref[...] = counts_ref[...] + used
    used = used.astype(jnp.bfloat16)
    total = sums_ref[...]
    for b in range(height // rows):
        part = own_ref[:, 0, b * rows : (b + 1) * rows, :].reshape(depth, LANES).astype(jnp.float32)
        part = part * part
        high = part.astype(jnp.bfloat16)
        low = (part - high.astype(jnp.float32)).astype(jnp.bfloat16)
        total = total + jnp.dot(used, high, preferred_element_type=jnp.float32)
        total = total + jnp.dot(used, low, preferred_element_type=jnp.float32)
    sums_ref[...] = total


def statistics(me, gates, own, top, cap):
    experts, holders, height, _ = own.shape
    depth = experts * GROUP * cap
    return pl.pallas_call(
        functools.partial(statistics_kernel, top=top, cap=cap),
        grid_spec=pltpu.PrefetchScalarGridSpec(
            num_scalar_prefetch=1,
            grid=(holders,),
            in_specs=[
                pl.BlockSpec((1,) + gates.shape[1:], lambda s, me: (s, 0, 0)),
                pl.BlockSpec((experts, 1, height, LANES), lambda s, me: (0, s, 0, 0)),
            ],
            out_specs=[
                pl.BlockSpec((experts, LANES), lambda s, me: (0, 0)),
                pl.BlockSpec((experts, depth), lambda s, me: (0, 0)),
            ],
        ),
        out_shape=[
            jax.ShapeDtypeStruct((experts, LANES), jnp.float32),
            jax.ShapeDtypeStruct((experts, depth), jnp.float32),
        ],
        name="statistics",
    )(me, gates, own)


def exchange(x, axis, size, bit):
    return lax.ppermute(x, axis, [(i, i ^ bit) for i in range(size)])


def body(dp, holders, expert_out, expert_ids, gate_weight):
    _, experts, _, cap, width = expert_out.shape
    tokens, top = expert_ids.shape
    tiles = width // LANES
    me = lax.axis_index("expert").astype(jnp.int32).reshape(1)
    own = expert_out.reshape(experts, holders, cap, tiles, LANES)
    own = own.transpose(0, 1, 3, 2, 4).reshape(experts, holders, tiles * cap, LANES)
    other = exchange(own, "expert", holders, 1)
    packed = jnp.concatenate([expert_ids.astype(jnp.float32), gate_weight], axis=1)
    gates = jnp.broadcast_to(packed[None], (holders,) + packed.shape)
    gates = lax.all_to_all(gates, "expert", split_axis=0, concat_axis=0, tiled=True)

    chips = holders // 2
    low = 1 << ((chips.bit_length() - 1) // 2)
    high = chips // low
    groups = tiles // GROUP
    cut = (groups + 1) // 2
    totals = []
    for first, last in ((0, cut), (cut, groups)):
        def part(digit):
            return combine(
                me, gates, own, other, lambda i: i * low + digit, high, first, last, top, cap
            )
        total = [part(d) for d in range(1, low)]
        moved = [exchange(t, "expert", holders, 2 * (d + 1)) for d, t in enumerate(total)]
        kept = part(0).astype(jnp.float32)
        for m in moved:
            kept = kept + m.astype(jnp.float32)
        kept = kept.astype(jnp.bfloat16)
        result = kept[0].astype(jnp.float32)
        for d in range(1, high):
            result = result + exchange(kept[d], "expert", holders, 2 * low * d).astype(jnp.float32)
        totals.append(result.astype(jnp.bfloat16))
    combined = jnp.concatenate(totals, axis=0).reshape(tiles, tokens, LANES)
    combined = combined.transpose(1, 0, 2).reshape(tokens, width)

    sums, counts = statistics(me, gates, own, top, cap)
    sums = jnp.sum(sums, axis=1)
    counts = jnp.sum(counts, axis=1) / GROUP
    both = jnp.stack([sums, counts])
    bit = 1
    while bit < dp:
        both = both + exchange(both, "dp", dp, bit)
        bit *= 2
    expert_rms = jnp.sqrt(both[0] / (both[1] * width) + epsilon)
    return combined, both[1].astype(jnp.int32), expert_rms


def solution(mesh):
    return jax.shard_map(
        functools.partial(body, mesh.shape["dp"], mesh.shape["expert"]),
        mesh=mesh,
        in_specs=(
            P("dp", "expert", None, None, None),
            P(("dp", "expert"), None),
            P(("dp", "expert"), None),
        ),
        out_specs=(P(("dp", "expert"), None), P("expert"), P("expert")),
        check_vma=False,
    )
```

time: 147 us -> 67.3 us (0.46)
  blocking collectives: 102 us -> 0 us
  Pallas kernels: 0 us -> 26.1 us
  local copies, waits for them, and re-layouts: 21.5 us -> 1.95 us
  waiting for transfers between devices: 0.01 us -> 11.4 us
  starting transfers between devices: 13.6 us -> 20.2 us
  matrix products: 2.32 us -> 0 us
    psum x1 -> x0, blocking collectives: 102 us -> none  [body(): lax.psum((sum_part, count_part), ('dp', 'expert'))]
    pallas_call x0 -> x5, Pallas kernels: none -> 26.1 us  [the longest x4 14.9 us: combine(): pl.pallas_call(kernel, out_shape=jax.ShapeDtypeStruct((count, rows * toke...]
    ppermute x0 -> x10, starting transfers between devices: none -> 13.2 us  [exchange(): return lax.ppermute(x, axis, [(i, i ^ bit) for i in range(size)])]
    reshape x3 -> x0, local copies, waits for them, and re-layouts: 8.62 us -> none  [the longest x1 8.4 us: body(): received = arrived.reshape(EXPERTS * CAP, width)]
    all_to_all x2 -> x1, starting transfers between devices: 13.6 us -> 7.04 us  [body(): lax.all_to_all(gates, 'expert', split_axis=0, concat_axis=0, tiled=True)]
    all_to_all x2 -> x1, waiting for transfers between devices: 0.01 us -> 6.36 us  [body(): lax.all_to_all(gates, 'expert', split_axis=0, concat_axis=0, tiled=True)]
    unnamed x5 -> x4, local copies, waits for them, and re-layouts: 7.26 us -> 1.41 us
    ppermute x0 -> x10, waiting for transfers between devices: none -> 5.09 us  [exchange(): return lax.ppermute(x, axis, [(i, i ^ bit) for i in range(size)])]
  transfers between devices with their start and end apart: 2 -> 11, of which waited for: 0 -> 5; matrix products, arithmetic and copies ran while one was open for 6% -> 11% of each run, Pallas kernels for 0% -> 34%
where the time goes in v1:
time: 67.3 us; the launch traced here: 66.5 us
  Pallas kernels  26.1 us (39%)
  starting transfers between devices  20.2 us (30%)
  waiting for transfers between devices  11.4 us (17%)
  other arithmetic  6.03 us (9%)
  local copies, waits for them, and re-layouts  1.95 us (3%)
  between operations  0.76 us (1%)
    pallas_call x4, Pallas kernels, combine(): pl.pallas_call(kernel, out_shape=jax.ShapeDtypeStruct((count, rows * toke...  14.9 us
    ppermute x10, starting transfers between devices, exchange(): return lax.ppermute(x, axis, [(i, i ^ bit) for i in range(size)])  13.2 us
    pallas_call x1, Pallas kernels, statistics(): pl.pallas_call(functools.partial(statistics_kernel, top=top, cap=cap), gr...  11.2 us
    all_to_all x1, starting transfers between devices, body(): lax.all_to_all(gates, 'expert', split_axis=0, concat_axis=0, tiled=True)  7.04 us
    all_to_all x1, waiting for transfers between devices, body(): lax.all_to_all(gates, 'expert', split_axis=0, concat_axis=0, tiled=True)  6.36 us
    ppermute x10, waiting for transfers between devices, exchange(): return lax.ppermute(x, axis, [(i, i ^ bit) for i in range(size)])  5.09 us
    unnamed x4, local copies, waits for them, and re-layouts  1.41 us
  transfers between devices with their start and end apart: 11, of which 5 were waited for; matrix products, arithmetic and copies ran while one was open for 11% of the time, Pallas kernels for 34%

profile of v1, /device:TPU:0, one launch (start us, length us, event | category | flops | bytes accessed | tf_op | source)
XLA Modules:
  0.0 66.5 jit_solution(14719968932585821025)
XLA Ops:
  1.2 0.7 %convert_element_type.63 = f32[8,8]{1,0:T(8,128)S(1)} convert(s32[8,8]{1,0:T(8,128)} %param.4) | non-fusion elementwise | flops 64 | bytes 512 | tf_op jit(solution)/shard_map/convert_element_type | solution.py:180
  1.9 0.8 %pad_maximum_fusion = f32[8,16]{1,0:T(8,128)S(1)} fusion(f32[8,8]{1,0:T(8,128)} %param.5, f32[8,8]{1,0:T(8,128)S(1)} %convert_element_type.63), kind=kLoop, calls=%fused_computation.19 | loop fusion | flops 128 | bytes 1024 | tf_op jit(solution)/shard_map/concatenate | solution.py:180
  2.6 0.7 %reshape.49 = f32[16,1,128]{2,1,0:T(1,128)} reshape(f32[16,8,16]{2,1,0:T(8,128)S(1)} %broadcast_in_dim.2) | data formatting | bytes 16384
  3.3 7.0 %all-to-all-start = ((f32[16,1,128]{2,1,0:T(1,128)}), f32[16,1,128]{2,1,0:T(1,128)S(1)}, u32[]{:S(2)}, u32[]{:S(2)}) async-start(f32[16,1,128]{2,1,0:T(1,128)} %reshape.49), calls=%async_computation | async-start | bytes 16384 | tf_op jit(solution)/shard_map/all_to_all | solution.py:182
  10.4 6.4 %all-to-all-done = f32[16,1,128]{2,1,0:T(1,128)S(1)} async-done(((f32[16,1,128]{2,1,0:T(1,128)}), f32[16,1,128]{2,1,0:T(1,128)S(1)}, u32[]{:S(2)}, u32[]{:S(2)}) %all-to-all-start) | async-done | bytes 8224 | tf_op jit(solution)/shard_map/all_to_all | solution.py:182
  17.3 0.7 %reduce = f32[16,128]{1,0:T(8,128)S(1)} reduce(f32[16,1,128]{2,1,0:T(1,128)S(1)} %all-to-all-done, f32[]{:T(128)} %broadcast.30), dimensions={1}, to_apply=%all_to_all.3.reduce_sub_computation | reduce | bytes 16388 | tf_op jit(solution)/shard_map/all_to_all | solution.py:182
  17.9 0.7 %reshape.50.gates_ref = f32[16,8,16]{2,1,0:T(8,128)} reshape(f32[16,128]{1,0:T(8,128)S(1)} %reduce) | data formatting | bytes 16384
  18.6 11.2 %statistics.1 = (f32[8,128]{1,0:T(8,128)}, f32[8,128]{1,0:T(8,128)}) custom-call(s32[1]{0:T(128)} %bitcast.me_ref, f32[16,8,16]{2,1,0:T(8,128)} %reshape.50.gates_ref, bf16[8,16,112,128]{3,2,1,0:T(8,128)(2,1)} %bitcast.42), custom_call_target="tpu_custom_call" | custom-call | tf_op jit(solution)/shard_map/statistics/pallas_call | solution.py:146
  29.8 0.8 %reduce_sum.19 = f32[8]{0:T(128)S(1)} reduce(f32[8,128]{1,0:T(8,128)} %get-tuple-element.6, f32[]{:T(128)} %constant.2.clone.1), dimensions={1}, to_apply=%region_1.0 | reduce | flops 1016 | bytes 4132 | tf_op jit(solution)/shard_map/reduce_sum | solution.py:210
  30.6 0.8 %reduce_sum.18 = f32[8]{0:T(128)S(1)} reduce(f32[8,128]{1,0:T(8,128)} %get-tuple-element.5, f32[]{:T(128)} %constant.2.clone.1), dimensions={1}, to_apply=%region_0.0 | reduce | flops 1016 | bytes 4132 | tf_op jit(solution)/shard_map/reduce_sum | solution.py:209
  31.4 1.6 %collective-permute-start.9 = (f32[2,8]{1,0:T(2,128)S(1)}, f32[2,8]{1,0:T(2,128)S(1)}, u32[]{:S(2)}, u32[]{:S(2)}) collective-permute-start(f32[2,8]{1,0:T(2,128)S(1)} %pad_maximum_fusion.1), channel_id=1, source_target_pairs={{0,16},{16,0},{1,17},{17,1},{2,18},{18,2},{3,19},{19,3},{4,20},{20... | collective-permute-start | bytes 200 | tf_op jit(solution)/shard_map/ppermute | solution.py:169
  33.0 2.1 %collective-permute-done.9 = f32[2,8]{1,0:T(2,128)S(1)} collective-permute-done((f32[2,8]{1,0:T(2,128)S(1)}, f32[2,8]{1,0:T(2,128)S(1)}, u32[]{:S(2)}, u32[]{:S(2)}) %collective-permute-start.9) | collective-permute-done | bytes 96 | tf_op jit(solution)/shard_map/ppermute | solution.py:169
  35.1 3.7 %combine.7 = bf16[4,192,128]{2,1,0:T(8,128)(2,1)} custom-call(s32[1]{0:T(128)} %bitcast.me_ref, f32[16,8,16]{2,1,0:T(8,128)} %reshape.50.gates_ref, bf16[8,16,112,128]{3,2,1,0:T(8,128)(2,1)} %bitcast.43, bf16[8,16,112,128]{3,2,1,0:T(8,128)(2,1)} %collective-permute-done.other_hbm), custom_call_target="tpu_custom_call" | custom-call | tf_op jit(solution)/shard_map/combine/pallas_call | solution.py:87
  39.9 3.8 %combine.5 = bf16[4,256,128]{2,1,0:T(8,128)(2,1)} custom-call(s32[1]{0:T(128)} %bitcast.me_ref, f32[16,8,16]{2,1,0:T(8,128)} %reshape.50.gates_ref, bf16[8,16,112,128]{3,2,1,0:T(8,128)(2,1)} %bitcast.44, bf16[8,16,112,128]{3,2,1,0:T(8,128)(2,1)} %collective-permute-done.other_hbm), custom_call_target="tpu_custom_call" | custom-call | tf_op jit(solution)/shard_map/combine/pallas_call | solution.py:87
  43.6 1.6 %collective-permute-start.1 = (bf16[4,256,128]{2,1,0:T(8,128)(2,1)}, bf16[4,256,128]{2,1,0:T(8,128)(2,1)S(1)}, u32[]{:S(2)}, u32[]{:S(2)}) collective-permute-start(bf16[4,256,128]{2,1,0:T(8,128)(2,1)} %combine.5), channel_id=1, source_target_pairs={{0,2},{1,3},{2,0},{3,1},{4,6},{5,7},{6,4},{7,5},{8,10},{9,11},{10,... | collective-permute-start | bytes 786440 | tf_op jit(solution)/shard_map/ppermute | solution.py:169
  45.2 3.8 %combine.4 = bf16[4,256,128]{2,1,0:T(8,128)(2,1)} custom-call(s32[1]{0:T(128)} %bitcast.me_ref, f32[16,8,16]{2,1,0:T(8,128)} %reshape.50.gates_ref, bf16[8,16,112,128]{3,2,1,0:T(8,128)(2,1)} %bitcast.45, bf16[8,16,112,128]{3,2,1,0:T(8,128)(2,1)} %collective-permute-done.other_hbm), custom_call_target="tpu_custom_call" | custom-call | tf_op jit(solution)/shard_map/combine/pallas_call | solution.py:87
  49.0 3.7 %combine.6 = bf16[4,192,128]{2,1,0:T(8,128)(2,1)} custom-call(s32[1]{0:T(128)} %bitcast.me_ref, f32[16,8,16]{2,1,0:T(8,128)} %reshape.50.gates_ref, bf16[8,16,112,128]{3,2,1,0:T(8,128)(2,1)} %bitcast.46, bf16[8,16,112,128]{3,2,1,0:T(8,128)(2,1)} %collective-permute-done.other_hbm), custom_call_target="tpu_custom_call" | custom-call | tf_op jit(solution)/shard_map/combine/pallas_call | solution.py:87
  52.7 1.0 %add_convert_fusion.1 = bf16[4,192,128]{2,1,0:T(8,128)(2,1)S(1)} fusion(bf16[4,192,128]{2,1,0:T(8,128)(2,1)S(1)} %collective-permute-done.5, bf16[4,192,128]{2,1,0:T(8,128)(2,1)} %combine.6), kind=kLoop, calls=%fused_computation.1 | loop fusion | flops 393216 | bytes 589824 | tf_op jit(solution)/shard_map/convert_element_type | solution.py:200
  54.9 3.3 %collective-permute-start.8 = (bf16[192,128]{1,0:T(8,128)(2,1)S(1)}, bf16[192,128]{1,0:T(8,128)(2,1)S(1)}, u32[]{:S(2)}, u32[]{:S(2)}) collective-permute-start(bf16[192,128]{1,0:T(8,128)(2,1)S(1)} %get-tuple-element.11), channel_id=1, source_target_pairs={{0,12},{1,13},{2,14},{3,15},{4,8},{5,9},{6,10},{7,11},{8,4},{9,5},... | collective-permute-start | bytes 147464 | tf_op jit(solution)/shard_map/ppermute | solution.py:169
  58.4 1.1 %collective-permute-start.3 = (bf16[256,128]{1,0:T(8,128)(2,1)S(1)}, bf16[256,128]{1,0:T(8,128)(2,1)S(1)}, u32[]{:S(2)}, u32[]{:S(2)}) collective-permute-start(bf16[256,128]{1,0:T(8,128)(2,1)S(1)} %get-tuple-element.9), channel_id=1, source_target_pairs={{0,8},{1,9},{2,10},{3,11},{4,12},{5,13},{6,14},{7,15},{8,0},{9,1},... | collective-permute-start | bytes 196616 | tf_op jit(solution)/shard_map/ppermute | solution.py:169
  59.5 3.3 %collective-permute-start.4 = (bf16[256,128]{1,0:T(8,128)(2,1)S(1)}, bf16[256,128]{1,0:T(8,128)(2,1)S(1)}, u32[]{:S(2)}, u32[]{:S(2)}) collective-permute-start(bf16[256,128]{1,0:T(8,128)(2,1)S(1)} %get-tuple-element.8), channel_id=1, source_target_pairs={{0,12},{1,13},{2,14},{3,15},{4,8},{5,9},{6,10},{7,11},{8,4},{9,5},... | collective-permute-start | bytes 196616 | tf_op jit(solution)/shard_map/ppermute | solution.py:169
  62.8 1.2 %collective-permute-done.2 = bf16[256,128]{1,0:T(8,128)(2,1)S(1)} collective-permute-done((bf16[256,128]{1,0:T(8,128)(2,1)S(1)}, bf16[256,128]{1,0:T(8,128)(2,1)S(1)}, u32[]{:S(2)}, u32[]{:S(2)}) %collective-permute-start.2) | collective-permute-done | bytes 65568 | tf_op jit(solution)/shard_map/ppermute | solution.py:169
  64.4 1.4 %collective-permute-done.4 = bf16[256,128]{1,0:T(8,128)(2,1)S(1)} collective-permute-done((bf16[256,128]{1,0:T(8,128)(2,1)S(1)}, bf16[256,128]{1,0:T(8,128)(2,1)S(1)}, u32[]{:S(2)}, u32[]{:S(2)}) %collective-permute-start.4) | collective-permute-done | bytes 65568 | tf_op jit(solution)/shard_map/ppermute | solution.py:169
  65.8 0.7 maximum_bitcast_fusion
  (25 shorter events, 4.0 us)
Async XLA Ops:
  0.6 34.4 %collective-permute-start = (bf16[8,16,112,128]{3,2,1,0:T(8,128)(2,1)}, bf16[8,16,112,128]{3,2,1,0:T(8,128)(2,1)}, u32[]{:S(2)}, u32[]{:S(2)}) collective-permute-start(bf16[8,16,112,128]{3,2,1,0:T(8,128)(2,1)} %bitcast.41), channel_id=1, source_target_pairs={{0,1},{1,0},{2,3},{3,2},{4,5},{5,4},{6,7},{7,6},{8,9},{9,8},{10,11... | collective-permute-start | bytes 11010056 | tf_op jit(solution)/shard_map/ppermute | solution.py:169
  3.3 13.4 %all-to-all-start = ((f32[16,1,128]{2,1,0:T(1,128)}), f32[16,1,128]{2,1,0:T(1,128)S(1)}, u32[]{:S(2)}, u32[]{:S(2)}) async-start(f32[16,1,128]{2,1,0:T(1,128)} %reshape.49), calls=%async_computation | async-start | bytes 16384 | tf_op jit(solution)/shard_map/all_to_all | solution.py:182
  31.4 3.6 %collective-permute-start.9 = (f32[2,8]{1,0:T(2,128)S(1)}, f32[2,8]{1,0:T(2,128)S(1)}, u32[]{:S(2)}, u32[]{:S(2)}) collective-permute-start(f32[2,8]{1,0:T(2,128)S(1)} %pad_maximum_fusion.1), channel_id=1, source_target_pairs={{0,16},{16,0},{1,17},{17,1},{2,18},{18,2},{3,19},{19,3},{4,20},{20... | collective-permute-start | bytes 200 | tf_op jit(solution)/shard_map/ppermute | solution.py:169
  38.8 14.0 %collective-permute-start.5 = (bf16[4,192,128]{2,1,0:T(8,128)(2,1)}, bf16[4,192,128]{2,1,0:T(8,128)(2,1)S(1)}, u32[]{:S(2)}, u32[]{:S(2)}) collective-permute-start(bf16[4,192,128]{2,1,0:T(8,128)(2,1)} %combine.7), channel_id=1, source_target_pairs={{0,2},{1,3},{2,0},{3,1},{4,6},{5,7},{6,4},{7,5},{8,10},{9,11},{10,... | collective-permute-start | bytes 589832 | tf_op jit(solution)/shard_map/ppermute | solution.py:169
  43.6 14.6 %collective-permute-start.1 = (bf16[4,256,128]{2,1,0:T(8,128)(2,1)}, bf16[4,256,128]{2,1,0:T(8,128)(2,1)S(1)}, u32[]{:S(2)}, u32[]{:S(2)}) collective-permute-start(bf16[4,256,128]{2,1,0:T(8,128)(2,1)} %combine.5), channel_id=1, source_target_pairs={{0,2},{1,3},{2,0},{3,1},{4,6},{5,7},{6,4},{7,5},{8,10},{9,11},{10,... | collective-permute-start | bytes 786440 | tf_op jit(solution)/shard_map/ppermute | solution.py:169
  49.0 9.2 %copy-start = (bf16[4,256,128]{2,1,0:T(8,128)(2,1)S(1)}, bf16[4,256,128]{2,1,0:T(8,128)(2,1)}, u32[]{:S(2)}) copy-start(bf16[4,256,128]{2,1,0:T(8,128)(2,1)} %combine.4) | copy-start | bytes 786436
  53.7 5.7 %collective-permute-start.6 = (bf16[192,128]{1,0:T(8,128)(2,1)S(1)}, bf16[192,128]{1,0:T(8,128)(2,1)S(1)}, u32[]{:S(2)}, u32[]{:S(2)}) collective-permute-start(bf16[192,128]{1,0:T(8,128)(2,1)S(1)} %get-tuple-element.10), channel_id=1, source_target_pairs={{0,4},{1,5},{2,6},{3,7},{4,0},{5,1},{6,2},{7,3},{8,12},{9,13},{10,... | collective-permute-start | bytes 147464 | tf_op jit(solution)/shard_map/ppermute | solution.py:169
  54.3 8.4 %collective-permute-start.7 = (bf16[192,128]{1,0:T(8,128)(2,1)S(1)}, bf16[192,128]{1,0:T(8,128)(2,1)S(1)}, u32[]{:S(2)}, u32[]{:S(2)}) collective-permute-start(bf16[192,128]{1,0:T(8,128)(2,1)S(1)} %get-tuple-element.12), channel_id=1, source_target_pairs={{0,8},{1,9},{2,10},{3,11},{4,12},{5,13},{6,14},{7,15},{8,0},{9,1},... | collective-permute-start | bytes 147464 | tf_op jit(solution)/shard_map/ppermute | solution.py:169
  54.9 7.8 %collective-permute-start.8 = (bf16[192,128]{1,0:T(8,128)(2,1)S(1)}, bf16[192,128]{1,0:T(8,128)(2,1)S(1)}, u32[]{:S(2)}, u32[]{:S(2)}) collective-permute-start(bf16[192,128]{1,0:T(8,128)(2,1)S(1)} %get-tuple-element.11), channel_id=1, source_target_pairs={{0,12},{1,13},{2,14},{3,15},{4,8},{5,9},{6,10},{7,11},{8,4},{9,5},... | collective-permute-start | bytes 147464 | tf_op jit(solution)/shard_map/ppermute | solution.py:169
  58.3 5.7 %collective-permute-start.2 = (bf16[256,128]{1,0:T(8,128)(2,1)S(1)}, bf16[256,128]{1,0:T(8,128)(2,1)S(1)}, u32[]{:S(2)}, u32[]{:S(2)}) collective-permute-start(bf16[256,128]{1,0:T(8,128)(2,1)S(1)} %get-tuple-element.7), channel_id=1, source_target_pairs={{0,4},{1,5},{2,6},{3,7},{4,0},{5,1},{6,2},{7,3},{8,12},{9,13},{10,... | collective-permute-start | bytes 196616 | tf_op jit(solution)/shard_map/ppermute | solution.py:169
  58.4 6.0 %collective-permute-start.3 = (bf16[256,128]{1,0:T(8,128)(2,1)S(1)}, bf16[256,128]{1,0:T(8,128)(2,1)S(1)}, u32[]{:S(2)}, u32[]{:S(2)}) collective-permute-start(bf16[256,128]{1,0:T(8,128)(2,1)S(1)} %get-tuple-element.9), channel_id=1, source_target_pairs={{0,8},{1,9},{2,10},{3,11},{4,12},{5,13},{6,14},{7,15},{8,0},{9,1},... | collective-permute-start | bytes 196616 | tf_op jit(solution)/shard_map/ppermute | solution.py:169
  59.5 6.3 %collective-permute-start.4 = (bf16[256,128]{1,0:T(8,128)(2,1)S(1)}, bf16[256,128]{1,0:T(8,128)(2,1)S(1)}, u32[]{:S(2)}, u32[]{:S(2)}) collective-permute-start(bf16[256,128]{1,0:T(8,128)(2,1)S(1)} %get-tuple-element.8), channel_id=1, source_target_pairs={{0,12},{1,13},{2,14},{3,15},{4,8},{5,9},{6,10},{7,11},{8,4},{9,5},... | collective-permute-start | bytes 196616 | tf_op jit(solution)/shard_map/ppermute | solution.py:169

commit v2 on v0

v2 whole, which is shorter than its diff:
```python
import functools

import jax
import jax.numpy as jnp
from jax import lax
from jax.experimental import pallas as pl
from jax.experimental.pallas import tpu as pltpu
from jax.sharding import PartitionSpec as P


LANES = 128
GROUP = 8

epsilon = 1e-06

VMEM = pl.BlockSpec(memory_space=pltpu.VMEM)
SMEM = pl.BlockSpec(memory_space=pltpu.SMEM)
HBM = pl.BlockSpec(memory_space=pltpu.HBM)


def iota(shape, axis):
    return lax.broadcasted_iota(jnp.int32, shape, axis)


def params():
    return pltpu.CompilerParams(vmem_limit_bytes=16 << 20)


def near(x):
    return pltpu.with_memory_space_constraint(x, pltpu.VMEM)


def far(x):
    return pltpu.with_memory_space_constraint(x, pltpu.HBM)


def split(x):
    high = x.astype(jnp.bfloat16)
    return high, (x - high.astype(jnp.float32)).astype(jnp.bfloat16)


def weights_kernel(ids_hbm, gates_hbm, out_ref, ids_ref, gates_ref, sems):
    loads = [
        pltpu.make_async_copy(ids_hbm, ids_ref, sems.at[0]),
        pltpu.make_async_copy(gates_hbm, gates_ref, sems.at[1]),
    ]
    for copy in loads:
        copy.start()
    for copy in loads:
        copy.wait()
    _, tokens, experts = out_ref.shape
    ids, gates = ids_ref[...], gates_ref[...]
    shape = (tokens, experts)
    lane, row = iota(shape, 1), iota(shape, 0)
    gate = jnp.zeros(shape, jnp.float32)
    named = jnp.zeros(shape, jnp.float32)
    for k in range(ids.shape[1]):
        same = jnp.broadcast_to(ids[:, k : k + 1], shape) == lane
        named = jnp.where(same, 1.0, named)
        gate = jnp.where(same, jnp.broadcast_to(gates[:, k : k + 1], shape), gate)
    upto, shift = named, 1
    while shift < tokens:
        upto = upto + jnp.where(row >= shift, pltpu.roll(upto, shift, 0), 0.0)
        shift *= 2
    signed = jnp.where(upto - named > 0.5, -gate, gate)
    out_ref[...] = jnp.broadcast_to(signed[None], out_ref.shape)


def weights(ids, gates, holders, experts):
    return pl.pallas_call(
        weights_kernel,
        out_shape=pltpu.VMEM((holders, ids.shape[0], experts), jnp.float32),
        in_specs=[HBM, HBM],
        out_specs=VMEM,
        scratch_shapes=[
            pltpu.VMEM(ids.shape, ids.dtype),
            pltpu.VMEM(gates.shape, gates.dtype),
            pltpu.SemaphoreType.DMA((2,)),
        ],
        compiler_params=params(),
        name="weights",
    )(far(ids), far(gates))


def prepare_kernel(me_ref, own_hbm, other_hbm, squares_ref, send_ref, own_ref, sems, send_sems, *, sources):
    me = me_ref[0]
    experts, holders, height, _ = own_hbm.shape
    loads = [pltpu.make_async_copy(own_hbm.at[e], own_ref.at[e], sems.at[e]) for e in range(experts)]
    for copy in loads:
        copy.start()
    sends = []
    for i, q in enumerate(sources):
        source = ((me >> 1) ^ q) * 2 + (me & 1)
        for h, ref in enumerate((own_hbm, other_hbm)):
            sends.append(pltpu.make_async_copy(ref.at[:, source], send_ref.at[i, h], send_sems.at[i, h]))
    for copy in sends:
        copy.start()
    ones = jnp.ones((8, LANES), jnp.bfloat16)
    for e in range(experts):
        loads[e].wait()
        parts = []
        for s in range(holders):
            total = jnp.zeros((8, LANES), jnp.float32)
            for r in range(0, height, 16):
                part = own_ref[e, s, r : r + 16, :].astype(jnp.float32)
                total = total + part[:8] * part[:8] + part[8:] * part[8:]
            parts.append(total)
        total = jnp.concatenate(parts, axis=0)
        sums = jnp.zeros((8, holders * 8), jnp.float32)
        for term in split(total):
            sums = sums + lax.dot_general(
                ones, term, (((1,), (1,)), ((), ())), preferred_element_type=jnp.float32
            )
        squares_ref[e] = sums
    for copy in sends:
        copy.wait()


def prepare(me, own, other, sources):
    experts, holders, height, _ = own.shape
    return pl.pallas_call(
        functools.partial(prepare_kernel, sources=sources),
        in_specs=[SMEM, HBM, HBM],
        out_specs=[VMEM, VMEM],
        out_shape=[
            pltpu.VMEM((experts, 8, holders * 8), jnp.float32),
            pltpu.VMEM((len(sources), 2, experts, height, LANES), own.dtype),
        ],
        scratch_shapes=[
            pltpu.VMEM(own.shape, own.dtype),
            pltpu.SemaphoreType.DMA((experts,)),
            pltpu.SemaphoreType.DMA((len(sources), 2)),
        ],
        compiler_params=params(),
        name="prepare",
    )(me, far(own), far(other))


def statistics_kernel(me_ref, signed_ref, squares_ref, out_ref, *, cap):
    holders, _, every = signed_ref.shape
    experts = squares_ref.shape[0]
    wide = squares_ref.shape[2]
    signed = signed_ref[...]
    mine = jnp.where(
        iota((experts, every), 1) == me_ref[0] * experts + iota((experts, every), 0), 1.0, 0.0
    ).astype(jnp.bfloat16)
    spread = iota((holders, wide), 1) // 8 == iota((holders, wide), 0)
    slot = iota((experts, wide), 1) % cap
    row = iota((experts, wide), 0)
    total = jnp.zeros((experts, wide), jnp.float32)
    for c, used in enumerate((signed > 0.0, signed < 0.0)):
        used = jnp.max(jnp.where(used, 1.0, 0.0), axis=1).astype(jnp.bfloat16)
        used = lax.dot_general(
            mine, used, (((1,), (1,)), ((), ())), preferred_element_type=jnp.float32
        )
        used = jnp.dot(
            used.astype(jnp.bfloat16),
            jnp.where(spread, 1.0, 0.0).astype(jnp.bfloat16),
            preferred_element_type=jnp.float32,
        )
        total = jnp.where(slot == c, used, total)
    square = jnp.zeros((experts, wide), jnp.float32)
    for e in range(experts):
        square = jnp.where(row == e, jnp.broadcast_to(squares_ref[e, 0:1, :], square.shape), square)
    sums = jnp.sum(total * square, axis=1, keepdims=True)
    counts = jnp.sum(total, axis=1, keepdims=True) * (cap / 8)
    out_ref[...] = jnp.where(iota(out_ref.shape, 1) < LANES // 2, sums, counts)


def statistics(me, signed, square, cap):
    return pl.pallas_call(
        functools.partial(statistics_kernel, cap=cap),
        out_shape=pltpu.VMEM((square.shape[0], LANES), jnp.float32),
        in_specs=[SMEM, VMEM, VMEM],
        out_specs=VMEM,
        compiler_params=params(),
        name="statistics",
    )(me, near(signed), near(square))


def lefts(me, signed_ref, source, experts, cap):
    tokens, every = signed_ref.shape[1:]
    rows = GROUP * cap
    depth = 2 * experts * rows
    lane = iota((every, depth), 1)
    holder = jnp.where(lane < experts * rows, me, me ^ 1)
    chosen = iota((every, depth), 0) == holder * experts + (lane // rows) % experts
    chosen = jnp.where(chosen, 1.0, 0.0).astype(jnp.bfloat16)
    signed = jnp.concatenate([signed_ref[s] for s in source], axis=0)
    high, low = split(signed)
    high = jnp.dot(high, chosen, preferred_element_type=jnp.float32)
    low = jnp.dot(low, chosen, preferred_element_type=jnp.float32)
    second = high < 0.0
    keep = second == (iota(high.shape, 1) % cap == 1)
    sign = jnp.where(second, -1.0, 1.0)
    high = jnp.where(keep, high * sign, 0.0)
    low = jnp.where(keep, low * sign, 0.0)
    tile = (iota((tokens, depth), 1) // cap) % GROUP
    for i in range(len(source)):
        span = slice(i * tokens, (i + 1) * tokens)
        left = [jnp.where(tile == j, term[span], 0.0) for term in (high, low) for j in range(GROUP)]
        yield jnp.concatenate(left, axis=0).astype(jnp.bfloat16)


def weighted(left, part):
    total = jnp.dot(left, part.reshape(-1, LANES), preferred_element_type=jnp.float32)
    half = left.shape[0] // 2
    return total[:half] + total[half:]


def send_kernel(me_ref, signed_ref, rows_ref, out_ref, *, sources, first, last, cap):
    me = me_ref[0]
    rows, high = GROUP * cap, GROUP * signed_ref.shape[1]
    source = [((me >> 1) ^ q) * 2 + (me & 1) for q in sources]
    for i, left in enumerate(lefts(me, signed_ref, source, rows_ref.shape[2], cap)):
        for b in range(last - first):
            total = weighted(left, rows_ref[i, :, :, (first + b) * rows : (first + b + 1) * rows, :])
            out_ref[i, b * high : (b + 1) * high, :] = total.astype(out_ref.dtype)


def send(me, signed, rows, sources, first, last, cap):
    height = (last - first) * GROUP * signed.shape[1]
    return pl.pallas_call(
        functools.partial(send_kernel, sources=sources, first=first, last=last, cap=cap),
        out_shape=pltpu.VMEM((len(sources), height, LANES), rows.dtype),
        in_specs=[SMEM, VMEM, VMEM],
        out_specs=VMEM,
        compiler_params=params(),
        name="send",
    )(me, near(signed), near(rows))


def keep_kernel(me_ref, signed_ref, own_hbm, other_hbm, out_ref, buffer, sems, *, sources, cap):
    me = me_ref[0]
    rows, high = GROUP * cap, GROUP * signed_ref.shape[1]
    source = [((me >> 1) ^ q) * 2 + (me & 1) for q in sources]
    copies = [
        [
            pltpu.make_async_copy(ref.at[:, s], buffer.at[i, h], sems.at[i, h])
            for h, ref in enumerate((own_hbm, other_hbm))
        ]
        for i, s in enumerate(source)
    ]
    for pair in copies:
        for copy in pair:
            copy.start()
    for i, left in enumerate(lefts(me, signed_ref, source, own_hbm.shape[0], cap)):
        for copy in copies[i]:
            copy.wait()
        for b in range(own_hbm.shape[2] // rows):
            total = weighted(left, buffer[i, :, :, b * rows : (b + 1) * rows, :])
            out_ref[i, b * high : (b + 1) * high, :] = total


def keep(me, signed, own, other, sources, cap):
    experts, _, height, _ = own.shape
    return pl.pallas_call(
        functools.partial(keep_kernel, sources=sources, cap=cap),
        out_shape=pltpu.VMEM((len(sources), height // cap * signed.shape[1], LANES), jnp.float32),
        in_specs=[SMEM, VMEM, HBM, HBM],
        out_specs=VMEM,
        scratch_shapes=[
            pltpu.VMEM((len(sources), 2, experts, height, LANES), own.dtype),
            pltpu.SemaphoreType.DMA((len(sources), 2)),
        ],
        compiler_params=params(),
        name="keep",
    )(me, near(signed), far(own), far(other))


def exchange(x, axis, size, bit):
    return lax.ppermute(x, axis, [(i, i ^ bit) for i in range(size)])


def body(dp, holders, expert_out, expert_ids, gate_weight):
    _, experts, _, cap, width = expert_out.shape
    tokens = expert_ids.shape[0]
    tiles = width // LANES
    me = lax.axis_index("expert").astype(jnp.int32).reshape(1)
    own = expert_out.reshape(experts, holders, cap, tiles, LANES)
    own = own.transpose(0, 1, 3, 2, 4).reshape(experts, holders, tiles * cap, LANES)
    other = exchange(own, "expert", holders, 1)
    signed = weights(expert_ids, gate_weight, holders, experts * holders)
    signed = lax.all_to_all(signed, "expert", split_axis=0, concat_axis=0, tiled=True)
    chips = holders // 2
    low = 1 << ((chips.bit_length() - 1) // 2)
    high = chips // low
    groups = tiles // GROUP
    cut = (groups + 1) // 2
    sources = [[i * low + digit for i in range(high)] for digit in range(low)]
    square, rows = prepare(me, own, other, [q for some in sources[1:] for q in some])
    chunks = ((0, cut), (cut, groups))
    moved = []
    for first, last in chunks:
        part = send(me, signed, rows, [q for some in sources[1:] for q in some], first, last, cap)
        part = part.reshape(low - 1, high, -1, LANES)
        moved.append([exchange(part[d - 1], "expert", holders, 2 * d) for d in range(1, low)])
    kept = keep(me, signed, own, other, sources[0], cap)
    totals = []
    for (first, last), some in zip(chunks, moved):
        total = kept[:, first * GROUP * tokens : last * GROUP * tokens]
        for m in some:
            total = total + m.astype(jnp.float32)
        result = total[0]
        for d in range(1, high):
            m = exchange(total[d].astype(jnp.bfloat16), "expert", holders, 2 * low * d)
            result = result + m.astype(jnp.float32)
        totals.append(result.astype(jnp.bfloat16))
    combined = jnp.concatenate(totals, axis=0).reshape(tiles, tokens, LANES)
    combined = combined.transpose(1, 0, 2).reshape(tokens, width)

    both = statistics(me, signed, square, cap)
    bit = 1
    while bit < dp:
        other = exchange(both, "dp", dp, bit)
        both = both + other
        bit *= 2
    sums, counts = both[:, 0], both[:, LANES - 1]
    expert_rms = jnp.sqrt(sums / (counts * width) + epsilon)
    counts = counts.astype(jnp.int32)
    return combined, counts, expert_rms


def solution(mesh):
    def step(*args):
        return body(mesh.shape["dp"], mesh.shape["expert"], *args)

    step = jax.shard_map(
        step,
        mesh=mesh,
        in_specs=(
            P("dp", "expert", None, None, None),
            P(("dp", "expert"), None),
            P(("dp", "expert"), None),
        ),
        out_specs=(P(("dp", "expert"), None), P("expert"), P("expert")),
        check_vma=False,
    )
    return step
```

time: 147 us -> 40.9 us (0.28)
  blocking collectives: 102 us -> 0 us
  local copies, waits for them, and re-layouts: 21.5 us -> 0.03 us
  waiting for transfers between devices: 0.01 us -> 10.8 us
  Pallas kernels: 0 us -> 8.44 us
  starting transfers between devices: 13.6 us -> 18.4 us
  other arithmetic: 6.91 us -> 2.25 us
  matrix products: 2.32 us -> 0 us
    psum x1 -> x0, blocking collectives: 102 us -> none  [body(): lax.psum((sum_part, count_part), ('dp', 'expert'))]
    ppermute x0 -> x10, starting transfers between devices: none -> 11.3 us  [exchange(): return lax.ppermute(x, axis, [(i, i ^ bit) for i in range(size)])]
    reshape x3 -> x0, local copies, waits for them, and re-layouts: 8.62 us -> none  [the longest x1 8.4 us: body(): received = arrived.reshape(EXPERTS * CAP, width)]
    pallas_call x0 -> x6, Pallas kernels: none -> 8.44 us  [the longest x1 3.22 us: prepare(): pl.pallas_call(functools.partial(prepare_kernel, sources=sources), in_spe...]
    unnamed x5 -> x0, local copies, waits for them, and re-layouts: 7.26 us -> none
    ppermute x0 -> x10, waiting for transfers between devices: none -> 7.12 us  [exchange(): return lax.ppermute(x, axis, [(i, i ^ bit) for i in range(size)])]
    all_to_all x2 -> x1, starting transfers between devices: 13.6 us -> 7.05 us  [body(): lax.all_to_all(signed, 'expert', split_axis=0, concat_axis=0, tiled=True)]
    reduce_sum x4 -> x0, other arithmetic: 6.26 us -> none  [the longest x1 5.9 us: body(): local_squares = jnp.sum(jnp.square(expert_out.astype(jnp.float32)), axis=4)]
  transfers between devices with their start and end apart: 2 -> 11, of which waited for: 0 -> 7; matrix products, arithmetic and copies ran while one was open for 6% -> 4% of each run, Pallas kernels for 0% -> 17%
where the time goes in v2:
time: 40.9 us; the launch traced here: 40.6 us
  starting transfers between devices  18.4 us (45%)
  waiting for transfers between devices  10.8 us (26%)
  Pallas kernels  8.44 us (21%)
  other arithmetic  2.25 us (6%)
  between operations  0.75 us (2%)
    ppermute x10, starting transfers between devices, exchange(): return lax.ppermute(x, axis, [(i, i ^ bit) for i in range(size)])  11.3 us
    ppermute x10, waiting for transfers between devices, exchange(): return lax.ppermute(x, axis, [(i, i ^ bit) for i in range(size)])  7.12 us
    all_to_all x1, starting transfers between devices, body(): lax.all_to_all(signed, 'expert', split_axis=0, concat_axis=0, tiled=True)  7.05 us
    all_to_all x1, waiting for transfers between devices, body(): lax.all_to_all(signed, 'expert', split_axis=0, concat_axis=0, tiled=True)  3.65 us
    pallas_call x1, Pallas kernels, prepare(): pl.pallas_call(functools.partial(prepare_kernel, sources=sources), in_spe...  3.22 us
    pallas_call x1, Pallas kernels, keep(): pl.pallas_call(functools.partial(keep_kernel, sources=sources, cap=cap),...  2.29 us
    pallas_call x1, Pallas kernels, weights(): pl.pallas_call(weights_kernel, out_shape=pltpu.VMEM((holders, ids.shape[0...  1.45 us
    pallas_call x2, Pallas kernels, send(): pl.pallas_call(functools.partial(send_kernel, sources=sources, first=firs...  1.04 us
  transfers between devices with their start and end apart: 11, of which 7 were waited for; matrix products, arithmetic and copies ran while one was open for 4% of the time, Pallas kernels for 17%

profile of v2, /device:TPU:0, one launch (start us, length us, event | category | flops | bytes accessed | tf_op | source)
XLA Modules:
  0.0 40.6 jit_solution(7017288844926153167)
XLA Ops:
  0.6 0.6 %collective-permute-start = (bf16[8,16,112,128]{3,2,1,0:T(8,128)(2,1)}, bf16[8,16,112,128]{3,2,1,0:T(8,128)(2,1)}, u32[]{:S(2)}, u32[]{:S(2)}) collective-permute-start(bf16[8,16,112,128]{3,2,1,0:T(8,128)(2,1)} %bitcast.44), channel_id=1, source_target_pairs={{0,1},{1,0},{2,3},{3,2},{4,5},{5,4},{6,7},{7,6},{8,9},{9,8},{10,11... | collective-permute-start | bytes 11010056 | tf_op jit(solution)/shard_map/ppermute | solution.py:272
  1.2 1.4 %weights.1 = f32[16,8,128]{2,1,0:T(8,128)} custom-call(s32[8,8]{1,0:T(8,128)} %ids_hbm.1, f32[8,8]{1,0:T(8,128)} %gates_hbm.1), custom_call_target="tpu_custom_call" | custom-call | tf_op jit(solution)/shard_map/weights/pallas_call | solution.py:70
  2.6 7.0 %all-to-all-start = ((f32[16,8,128]{2,1,0:T(8,128)}), f32[16,8,128]{2,1,0:T(8,128)S(1)}, u32[]{:S(2)}, u32[]{:S(2)}) async-start(f32[16,8,128]{2,1,0:T(8,128)} %weights.1), calls=%async_computation | async-start | bytes 131072 | tf_op jit(solution)/shard_map/all_to_all | solution.py:284
  9.7 3.2 %prepare.1 = (f32[8,8,128]{2,1,0:T(8,128)S(1)}, bf16[4,2,8,112,128]{4,3,2,1,0:T(8,128)(2,1)S(1)}) custom-call(s32[1]{0:T(128)} %bitcast.me_ref, bf16[8,16,112,128]{3,2,1,0:T(8,128)(2,1)} %bitcast.45, bf16[8,16,112,128]{3,2,1,0:T(8,128)(2,1)} %collective-permute-done.other_hbm), custom_call_target="tpu_custom_call" | custom-call | tf_op jit(solution)/shard_map/prepare/pallas_call | solution.py:121
  12.9 3.7 %all-to-all-done.signed_ref = f32[16,8,128]{2,1,0:T(8,128)S(1)} async-done(((f32[16,8,128]{2,1,0:T(8,128)}), f32[16,8,128]{2,1,0:T(8,128)S(1)}, u32[]{:S(2)}, u32[]{:S(2)}) %all-to-all-start) | async-done | bytes 65568 | tf_op jit(solution)/shard_map/all_to_all | solution.py:284
  16.6 0.4 %statistics.1 = f32[8,128]{1,0:T(8,128)S(1)} custom-call(s32[1]{0:T(128)} %bitcast.me_ref, f32[16,8,128]{2,1,0:T(8,128)S(1)} %all-to-all-done.signed_ref, f32[8,8,128]{2,1,0:T(8,128)S(1)} %get-tuple-element.6.squares_ref), custom_call_target="tpu_custom_call" | custom-call | tf_op jit(solution)/shard_map/statistics/pallas_call | solution.py:171
  17.0 1.5 %collective-permute-start.9 = (f32[8,128]{1,0:T(8,128)S(1)}, f32[8,128]{1,0:T(8,128)S(1)}, u32[]{:S(2)}, u32[]{:S(2)}) collective-permute-start(f32[8,128]{1,0:T(8,128)S(1)} %statistics.1), channel_id=1, source_target_pairs={{0,16},{16,0},{1,17},{17,1},{2,18},{18,2},{3,19},{19,3},{4,20},{20... | collective-permute-start | bytes 12296 | tf_op jit(solution)/shard_map/ppermute | solution.py:272
  18.5 0.5 %send.3 = bf16[4,192,128]{2,1,0:T(8,128)(2,1)S(1)} custom-call(s32[1]{0:T(128)} %bitcast.me_ref, f32[16,8,128]{2,1,0:T(8,128)S(1)} %all-to-all-done.signed_ref, bf16[4,2,8,112,128]{4,3,2,1,0:T(8,128)(2,1)S(1)} %get-tuple-element.5.rows_ref), custom_call_target="tpu_custom_call" | custom-call | tf_op jit(solution)/shard_map/send/pallas_call | solution.py:223
  19.2 0.6 %send.2 = bf16[4,256,128]{2,1,0:T(8,128)(2,1)S(1)} custom-call(s32[1]{0:T(128)} %bitcast.me_ref, f32[16,8,128]{2,1,0:T(8,128)S(1)} %all-to-all-done.signed_ref, bf16[4,2,8,112,128]{4,3,2,1,0:T(8,128)(2,1)S(1)} %get-tuple-element.5.rows_ref), custom_call_target="tpu_custom_call" | custom-call | tf_op jit(solution)/shard_map/send/pallas_call | solution.py:223
  19.8 2.0 %collective-permute-start.1 = (bf16[4,256,128]{2,1,0:T(8,128)(2,1)S(1)}, bf16[4,256,128]{2,1,0:T(8,128)(2,1)S(1)}, u32[]{:S(2)}, u32[]{:S(2)}) collective-permute-start(bf16[4,256,128]{2,1,0:T(8,128)(2,1)S(1)} %send.2), channel_id=1, source_target_pairs={{0,2},{1,3},{2,0},{3,1},{4,6},{5,7},{6,4},{7,5},{8,10},{9,11},{10,... | collective-permute-start | bytes 786440 | tf_op jit(solution)/shard_map/ppermute | solution.py:272
  21.7 2.3 %keep.1 = f32[4,448,128]{2,1,0:T(8,128)S(1)} custom-call(s32[1]{0:T(128)} %bitcast.me_ref, f32[16,8,128]{2,1,0:T(8,128)S(1)} %all-to-all-done.signed_ref, bf16[8,16,112,128]{3,2,1,0:T(8,128)(2,1)} %bitcast.46, bf16[8,16,112,128]{3,2,1,0:T(8,128)(2,1)} %collective-permute-done.other_hbm), custom_call_target="tpu_custom_call" | custom-call | tf_op jit(solution)/shard_map/keep/pallas_call | solution.py:257
  24.1 0.7 %convert_reduce_fusion = s32[8]{0:T(128)} fusion(f32[8,128]{1,0:T(8,128)S(1)} %add.39), kind=kLoop, calls=%fused_computation.20 | loop fusion | flops 8 | bytes 64 | tf_op jit(solution)/shard_map/convert_element_type | solution.py:320
  24.8 0.7 %sqrt_reduce_fusion = f32[8]{0:T(128)} fusion(f32[8,128]{1,0:T(8,128)S(1)} %add.39), kind=kLoop, calls=%fused_computation.19 | loop fusion | flops 24 | bytes 96 | tf_op jit(solution)/shard_map/sqrt | solution.py:319
  25.5 1.4 %collective-permute-done.5 = bf16[4,192,128]{2,1,0:T(8,128)(2,1)S(1)} collective-permute-done((bf16[4,192,128]{2,1,0:T(8,128)(2,1)S(1)}, bf16[4,192,128]{2,1,0:T(8,128)(2,1)S(1)}, u32[]{:S(2)}, u32[]{:S(2)}) %collective-permute-start.5) | collective-permute-done | bytes 196640 | tf_op jit(solution)/shard_map/ppermute | solution.py:272
  27.1 1.6 %collective-permute-start.8 = (bf16[192,128]{1,0:T(8,128)(2,1)S(1)}, bf16[192,128]{1,0:T(8,128)(2,1)S(1)}, u32[]{:S(2)}, u32[]{:S(2)}) collective-permute-start(bf16[192,128]{1,0:T(8,128)(2,1)S(1)} %get-tuple-element.15), channel_id=1, source_target_pairs={{0,12},{1,13},{2,14},{3,15},{4,8},{5,9},{6,10},{7,11},{8,4},{9,5},... | collective-permute-start | bytes 147464 | tf_op jit(solution)/shard_map/ppermute | solution.py:272
  28.7 1.8 %collective-permute-start.7 = (bf16[192,128]{1,0:T(8,128)(2,1)S(1)}, bf16[192,128]{1,0:T(8,128)(2,1)S(1)}, u32[]{:S(2)}, u32[]{:S(2)}) collective-permute-start(bf16[192,128]{1,0:T(8,128)(2,1)S(1)} %get-tuple-element.16), channel_id=1, source_target_pairs={{0,8},{1,9},{2,10},{3,11},{4,12},{5,13},{6,14},{7,15},{8,0},{9,1},... | collective-permute-start | bytes 147464 | tf_op jit(solution)/shard_map/ppermute | solution.py:272
  30.9 0.8 %collective-permute-start.2 = (bf16[256,128]{1,0:T(8,128)(2,1)S(1)}, bf16[256,128]{1,0:T(8,128)(2,1)S(1)}, u32[]{:S(2)}, u32[]{:S(2)}) collective-permute-start(bf16[256,128]{1,0:T(8,128)(2,1)S(1)} %get-tuple-element.11), channel_id=1, source_target_pairs={{0,4},{1,5},{2,6},{3,7},{4,0},{5,1},{6,2},{7,3},{8,12},{9,13},{10,... | collective-permute-start | bytes 196616 | tf_op jit(solution)/shard_map/ppermute | solution.py:272
  31.7 1.6 %collective-permute-start.4 = (bf16[256,128]{1,0:T(8,128)(2,1)S(1)}, bf16[256,128]{1,0:T(8,128)(2,1)S(1)}, u32[]{:S(2)}, u32[]{:S(2)}) collective-permute-start(bf16[256,128]{1,0:T(8,128)(2,1)S(1)} %get-tuple-element.12), channel_id=1, source_target_pairs={{0,12},{1,13},{2,14},{3,15},{4,8},{5,9},{6,10},{7,11},{8,4},{9,5},... | collective-permute-start | bytes 196616 | tf_op jit(solution)/shard_map/ppermute | solution.py:272
  33.3 1.2 %collective-permute-start.3 = (bf16[256,128]{1,0:T(8,128)(2,1)S(1)}, bf16[256,128]{1,0:T(8,128)(2,1)S(1)}, u32[]{:S(2)}, u32[]{:S(2)}) collective-permute-start(bf16[256,128]{1,0:T(8,128)(2,1)S(1)} %get-tuple-element.13), channel_id=1, source_target_pairs={{0,8},{1,9},{2,10},{3,11},{4,12},{5,13},{6,14},{7,15},{8,0},{9,1},... | collective-permute-start | bytes 196616 | tf_op jit(solution)/shard_map/ppermute | solution.py:272
  34.5 0.4 collective-permute-done.7
  34.8 1.6 %collective-permute-done.2 = bf16[256,128]{1,0:T(8,128)(2,1)S(1)} collective-permute-done((bf16[256,128]{1,0:T(8,128)(2,1)S(1)}, bf16[256,128]{1,0:T(8,128)(2,1)S(1)}, u32[]{:S(2)}, u32[]{:S(2)}) %collective-permute-start.2) | collective-permute-done | bytes 65568 | tf_op jit(solution)/shard_map/ppermute | solution.py:272
  36.5 1.3 %collective-permute-done.4 = bf16[256,128]{1,0:T(8,128)(2,1)S(1)} collective-permute-done((bf16[256,128]{1,0:T(8,128)(2,1)S(1)}, bf16[256,128]{1,0:T(8,128)(2,1)S(1)}, u32[]{:S(2)}, u32[]{:S(2)}) %collective-permute-start.4) | collective-permute-done | bytes 65568 | tf_op jit(solution)/shard_map/ppermute | solution.py:272
  37.8 2.1 %collective-permute-done.3 = bf16[256,128]{1,0:T(8,128)(2,1)S(1)} collective-permute-done((bf16[256,128]{1,0:T(8,128)(2,1)S(1)}, bf16[256,128]{1,0:T(8,128)(2,1)S(1)}, u32[]{:S(2)}, u32[]{:S(2)}) %collective-permute-start.3) | collective-permute-done | bytes 65568 | tf_op jit(solution)/shard_map/ppermute | solution.py:272
  39.9 0.7 %maximum_bitcast_fusion = bf16[8,7168]{1,0:T(8,128)(2,1)} fusion(bf16[192,128]{1,0:T(8,128)(2,1)S(1)} %fusion.7, bf16[256,128]{1,0:T(8,128)(2,1)S(1)} %fusion.3), kind=kLoop, calls=%fused_computation.7 | loop fusion | flops 229376 | bytes 229376 | tf_op jit(solution)/shard_map/reshape | solution.py:310
  (14 shorter events, 0.9 us)
Async XLA Ops:
  0.6 9.1 %collective-permute-start = (bf16[8,16,112,128]{3,2,1,0:T(8,128)(2,1)}, bf16[8,16,112,128]{3,2,1,0:T(8,128)(2,1)}, u32[]{:S(2)}, u32[]{:S(2)}) collective-permute-start(bf16[8,16,112,128]{3,2,1,0:T(8,128)(2,1)} %bitcast.44), channel_id=1, source_target_pairs={{0,1},{1,0},{2,3},{3,2},{4,5},{5,4},{6,7},{7,6},{8,9},{9,8},{10,11... | collective-permute-start | bytes 11010056 | tf_op jit(solution)/shard_map/ppermute | solution.py:272
  2.6 14.0 %all-to-all-start = ((f32[16,8,128]{2,1,0:T(8,128)}), f32[16,8,128]{2,1,0:T(8,128)S(1)}, u32[]{:S(2)}, u32[]{:S(2)}) async-start(f32[16,8,128]{2,1,0:T(8,128)} %weights.1), calls=%async_computation | async-start | bytes 131072 | tf_op jit(solution)/shard_map/all_to_all | solution.py:284
  17.0 7.0 %collective-permute-start.9 = (f32[8,128]{1,0:T(8,128)S(1)}, f32[8,128]{1,0:T(8,128)S(1)}, u32[]{:S(2)}, u32[]{:S(2)}) collective-permute-start(f32[8,128]{1,0:T(8,128)S(1)} %statistics.1), channel_id=1, source_target_pairs={{0,16},{16,0},{1,17},{17,1},{2,18},{18,2},{3,19},{19,3},{4,20},{20... | collective-permute-start | bytes 12296 | tf_op jit(solution)/shard_map/ppermute | solution.py:272
  19.0 7.8 %collective-permute-start.5 = (bf16[4,192,128]{2,1,0:T(8,128)(2,1)S(1)}, bf16[4,192,128]{2,1,0:T(8,128)(2,1)S(1)}, u32[]{:S(2)}, u32[]{:S(2)}) collective-permute-start(bf16[4,192,128]{2,1,0:T(8,128)(2,1)S(1)} %send.3), channel_id=1, source_target_pairs={{0,2},{1,3},{2,0},{3,1},{4,6},{5,7},{6,4},{7,5},{8,10},{9,11},{10,... | collective-permute-start | bytes 589832 | tf_op jit(solution)/shard_map/ppermute | solution.py:272
  19.8 11.0 %collective-permute-start.1 = (bf16[4,256,128]{2,1,0:T(8,128)(2,1)S(1)}, bf16[4,256,128]{2,1,0:T(8,128)(2,1)S(1)}, u32[]{:S(2)}, u32[]{:S(2)}) collective-permute-start(bf16[4,256,128]{2,1,0:T(8,128)(2,1)S(1)} %send.2), channel_id=1, source_target_pairs={{0,2},{1,3},{2,0},{3,1},{4,6},{5,7},{6,4},{7,5},{8,10},{9,11},{10,... | collective-permute-start | bytes 786440 | tf_op jit(solution)/shard_map/ppermute | solution.py:272
  26.9 6.3 %collective-permute-start.6 = (bf16[192,128]{1,0:T(8,128)(2,1)S(1)}, bf16[192,128]{1,0:T(8,128)(2,1)S(1)}, u32[]{:S(2)}, u32[]{:S(2)}) collective-permute-start(bf16[192,128]{1,0:T(8,128)(2,1)S(1)} %get-tuple-element.14), channel_id=1, source_target_pairs={{0,4},{1,5},{2,6},{3,7},{4,0},{5,1},{6,2},{7,3},{8,12},{9,13},{10,... | collective-permute-start | bytes 147464 | tf_op jit(solution)/shard_map/ppermute | solution.py:272
  27.1 7.3 %collective-permute-start.8 = (bf16[192,128]{1,0:T(8,128)(2,1)S(1)}, bf16[192,128]{1,0:T(8,128)(2,1)S(1)}, u32[]{:S(2)}, u32[]{:S(2)}) collective-permute-start(bf16[192,128]{1,0:T(8,128)(2,1)S(1)} %get-tuple-element.15), channel_id=1, source_target_pairs={{0,12},{1,13},{2,14},{3,15},{4,8},{5,9},{6,10},{7,11},{8,4},{9,5},... | collective-permute-start | bytes 147464 | tf_op jit(solution)/shard_map/ppermute | solution.py:272
  28.7 6.1 %collective-permute-start.7 = (bf16[192,128]{1,0:T(8,128)(2,1)S(1)}, bf16[192,128]{1,0:T(8,128)(2,1)S(1)}, u32[]{:S(2)}, u32[]{:S(2)}) collective-permute-start(bf16[192,128]{1,0:T(8,128)(2,1)S(1)} %get-tuple-element.16), channel_id=1, source_target_pairs={{0,8},{1,9},{2,10},{3,11},{4,12},{5,13},{6,14},{7,15},{8,0},{9,1},... | collective-permute-start | bytes 147464 | tf_op jit(solution)/shard_map/ppermute | solution.py:272
  30.9 5.6 %collective-permute-start.2 = (bf16[256,128]{1,0:T(8,128)(2,1)S(1)}, bf16[256,128]{1,0:T(8,128)(2,1)S(1)}, u32[]{:S(2)}, u32[]{:S(2)}) collective-permute-start(bf16[256,128]{1,0:T(8,128)(2,1)S(1)} %get-tuple-element.11), channel_id=1, source_target_pairs={{0,4},{1,5},{2,6},{3,7},{4,0},{5,1},{6,2},{7,3},{8,12},{9,13},{10,... | collective-permute-start | bytes 196616 | tf_op jit(solution)/shard_map/ppermute | solution.py:272
  31.7 6.1 %collective-permute-start.4 = (bf16[256,128]{1,0:T(8,128)(2,1)S(1)}, bf16[256,128]{1,0:T(8,128)(2,1)S(1)}, u32[]{:S(2)}, u32[]{:S(2)}) collective-permute-start(bf16[256,128]{1,0:T(8,128)(2,1)S(1)} %get-tuple-element.12), channel_id=1, source_target_pairs={{0,12},{1,13},{2,14},{3,15},{4,8},{5,9},{6,10},{7,11},{8,4},{9,5},... | collective-permute-start | bytes 196616 | tf_op jit(solution)/shard_map/ppermute | solution.py:272
  33.3 6.7 %collective-permute-start.3 = (bf16[256,128]{1,0:T(8,128)(2,1)S(1)}, bf16[256,128]{1,0:T(8,128)(2,1)S(1)}, u32[]{:S(2)}, u32[]{:S(2)}) collective-permute-start(bf16[256,128]{1,0:T(8,128)(2,1)S(1)} %get-tuple-element.13), channel_id=1, source_target_pairs={{0,8},{1,9},{2,10},{3,11},{4,12},{5,13},{6,14},{7,15},{8,0},{9,1},... | collective-permute-start | bytes 196616 | tf_op jit(solution)/shard_map/ppermute | solution.py:272

commit v3 on v2

v3 whole, which is shorter than its diff:
```python
import functools

import jax
import jax.numpy as jnp
from jax import lax
from jax.experimental import pallas as pl
from jax.experimental.pallas import tpu as pltpu
from jax.sharding import PartitionSpec as P


LANES = 128
GROUP = 8

epsilon = 1e-06

VMEM = pl.BlockSpec(memory_space=pltpu.VMEM)
SMEM = pl.BlockSpec(memory_space=pltpu.SMEM)
HBM = pl.BlockSpec(memory_space=pltpu.HBM)


def iota(shape, axis):
    return lax.broadcasted_iota(jnp.int32, shape, axis)


def params():
    return pltpu.CompilerParams(vmem_limit_bytes=16 << 20)


def near(x):
    return pltpu.with_memory_space_constraint(x, pltpu.VMEM)


def far(x):
    return pltpu.with_memory_space_constraint(x, pltpu.HBM)


def split(x):
    high = x.astype(jnp.bfloat16)
    return high, (x - high.astype(jnp.float32)).astype(jnp.bfloat16)


def weights_kernel(ids_hbm, gates_hbm, out_ref, ids_ref, gates_ref, sems):
    loads = [
        pltpu.make_async_copy(ids_hbm, ids_ref, sems.at[0]),
        pltpu.make_async_copy(gates_hbm, gates_ref, sems.at[1]),
    ]
    for copy in loads:
        copy.start()
    for copy in loads:
        copy.wait()
    tokens = out_ref.shape[0]
    ids, gates = ids_ref[...], gates_ref[...]
    shape = out_ref.shape
    lane, row = iota(shape, 1), iota(shape, 0)
    gate = jnp.zeros(shape, jnp.float32)
    named = jnp.zeros(shape, jnp.float32)
    for k in range(ids.shape[1]):
        same = jnp.broadcast_to(ids[:, k : k + 1], shape) == lane
        named = jnp.where(same, 1.0, named)
        gate = jnp.where(same, jnp.broadcast_to(gates[:, k : k + 1], shape), gate)
    upto, shift = named, 1
    while shift < tokens:
        upto = upto + jnp.where(row >= shift, pltpu.roll(upto, shift, 0), 0.0)
        shift *= 2
    out_ref[...] = jnp.where(upto - named > 0.5, -gate, gate)


def weights(ids, gates, experts):
    return pl.pallas_call(
        weights_kernel,
        out_shape=pltpu.VMEM((ids.shape[0], experts), jnp.float32),
        in_specs=[HBM, HBM],
        out_specs=VMEM,
        scratch_shapes=[
            pltpu.VMEM(ids.shape, ids.dtype),
            pltpu.VMEM(gates.shape, gates.dtype),
            pltpu.SemaphoreType.DMA((2,)),
        ],
        compiler_params=params(),
        name="weights",
    )(far(ids), far(gates))


def load_kernel(own_hbm, own_ref, sem):
    copy = pltpu.make_async_copy(own_hbm, own_ref, sem)
    copy.start()
    copy.wait()


def load(own):
    return pl.pallas_call(
        load_kernel,
        out_shape=pltpu.VMEM(own.shape, own.dtype),
        in_specs=[HBM],
        out_specs=VMEM,
        scratch_shapes=[pltpu.SemaphoreType.DMA],
        compiler_params=params(),
        name="load",
    )(far(own))


def squares_kernel(own_ref, out_ref):
    experts, holders, height, _ = own_ref.shape
    ones = jnp.ones((8, LANES), jnp.bfloat16)
    for e in range(experts):
        parts = []
        for s in range(holders):
            total = jnp.zeros((8, LANES), jnp.float32)
            for r in range(0, height, 16):
                part = own_ref[e, s, r : r + 16, :].astype(jnp.float32)
                total = total + part[:8] * part[:8] + part[8:] * part[8:]
            parts.append(total)
        total = jnp.concatenate(parts, axis=0)
        sums = jnp.zeros((8, holders * 8), jnp.float32)
        for term in split(total):
            sums = sums + lax.dot_general(
                ones, term, (((1,), (1,)), ((), ())), preferred_element_type=jnp.float32
            )
        out_ref[e] = sums


def squares(own):
    experts, holders, _, _ = own.shape
    return pl.pallas_call(
        squares_kernel,
        out_shape=pltpu.VMEM((experts, 8, holders * 8), jnp.float32),
        in_specs=[VMEM],
        out_specs=VMEM,
        compiler_params=params(),
        name="squares",
    )(near(own))


def statistics_kernel(mine_ref, theirs_ref, squares_ref, out_ref, *, cap):
    me = lax.axis_index("expert")
    chips, _, every = mine_ref.shape
    experts, _, wide = squares_ref.shape
    mine = jnp.where(
        iota((experts, every), 1) == me * experts + iota((experts, every), 0), 1.0, 0.0
    ).astype(jnp.bfloat16)
    slot = iota((experts, wide), 1) % cap
    row = iota((experts, wide), 0)
    total = jnp.zeros((experts, wide), jnp.float32)
    for core, ref in enumerate((mine_ref, theirs_ref)):
        signed = ref[...]
        source = (iota((chips, wide), 0) * 2 + core) ^ me
        spread = jnp.where(iota((chips, wide), 1) // 8 == source, 1.0, 0.0).astype(jnp.bfloat16)
        for c, used in enumerate((signed > 0.0, signed < 0.0)):
            used = jnp.max(jnp.where(used, 1.0, 0.0), axis=1).astype(jnp.bfloat16)
            used = lax.dot_general(
                mine, used, (((1,), (1,)), ((), ())), preferred_element_type=jnp.float32
            )
            used = jnp.dot(used.astype(jnp.bfloat16), spread, preferred_element_type=jnp.float32)
            total = total + jnp.where(slot == c, used, 0.0)
    square = jnp.zeros((experts, wide), jnp.float32)
    for e in range(experts):
        square = jnp.where(row == e, jnp.broadcast_to(squares_ref[e, 0:1, :], square.shape), square)
    sums = jnp.sum(total * square, axis=1, keepdims=True)
    counts = jnp.sum(total, axis=1, keepdims=True) * (cap / 8)
    out_ref[...] = jnp.where(iota(out_ref.shape, 1) < LANES // 2, sums, counts)


def statistics(mine, theirs, square, cap):
    return pl.pallas_call(
        functools.partial(statistics_kernel, cap=cap),
        out_shape=pltpu.VMEM((square.shape[0], LANES), jnp.float32),
        in_specs=[VMEM, VMEM, VMEM],
        out_specs=VMEM,
        compiler_params=params(),
        name="statistics",
    )(near(mine), near(theirs), near(square))


def combine_kernel(signed_ref, own_ref, other_ref, out_ref, *, sources, first, last, cap):
    me = lax.axis_index("expert")
    experts = own_ref.shape[0]
    tokens, every = signed_ref.shape[1:]
    rows = GROUP * cap
    depth = 2 * experts * rows
    lane = iota((every, depth), 1)
    holder = jnp.where(lane < experts * rows, me, me ^ 1)
    chosen = iota((every, depth), 0) == holder * experts + (lane // rows) % experts
    chosen = jnp.where(chosen, 1.0, 0.0).astype(jnp.bfloat16)
    signed = signed_ref[...].reshape(-1, every)
    high, low = split(signed)
    high = jnp.dot(high, chosen, preferred_element_type=jnp.float32)
    low = jnp.dot(low, chosen, preferred_element_type=jnp.float32)
    second = high < 0.0
    kept = second == (iota(high.shape, 1) % cap == 1)
    sign = jnp.where(second, -1.0, 1.0)
    high = jnp.where(kept, high * sign, 0.0)
    low = jnp.where(kept, low * sign, 0.0)
    tile = (iota((tokens, depth), 1) // cap) % GROUP
    half = GROUP * tokens
    for i, q in enumerate(sources):
        source = me ^ (2 * q)
        span = slice(i * tokens, (i + 1) * tokens)
        left = [jnp.where(tile == j, term[span], 0.0) for term in (high, low) for j in range(GROUP)]
        left = jnp.concatenate(left, axis=0).astype(jnp.bfloat16)
        for b in range(first, last):
            part = slice(b * rows, (b + 1) * rows)
            part = jnp.concatenate([own_ref[:, source, part, :], other_ref[:, source, part, :]], axis=0)
            total = jnp.dot(left, part.reshape(depth, LANES), preferred_element_type=jnp.float32)
            total = total[:half] + total[half:]
            out_ref[i, (b - first) * half : (b - first + 1) * half, :] = total.astype(out_ref.dtype)


def combine(signed, own, other, sources, first, last, cap, dtype):
    rows = (last - first) * GROUP
    return pl.pallas_call(
        functools.partial(combine_kernel, sources=sources, first=first, last=last, cap=cap),
        out_shape=pltpu.VMEM((len(sources), rows * signed.shape[1], LANES), dtype),
        in_specs=[VMEM, VMEM, VMEM],
        out_specs=VMEM,
        compiler_params=params(),
    )(near(signed), near(own), near(other))


def exchange(x, axis, size, bit):
    return lax.ppermute(x, axis, [(i, i ^ bit) for i in range(size)])


def body(dp, holders, expert_out, expert_ids, gate_weight):
    _, experts, _, cap, width = expert_out.shape
    tokens = expert_ids.shape[0]
    tiles = width // LANES
    groups = tiles // GROUP
    chips = holders // 2
    low = 1 << ((chips.bit_length() - 1) // 2)
    high = chips // low

    def swap(x, bit):
        return exchange(x, "expert", holders, bit)

    own = expert_out.reshape(experts, holders, cap, tiles, LANES)
    own = own.transpose(0, 1, 3, 2, 4).reshape(experts, holders, tiles * cap, LANES)
    other = swap(own, 1)
    tile = weights(expert_ids, gate_weight, experts * holders)
    signed = jnp.stack([tile] + [swap(tile, 2 * d) for d in range(1, low)])
    own = load(own)
    signed = [signed]
    for h in range(1, high):
        signed.append(swap(signed[0], 2 * low * h))

    def sums(pairs, first, last, dtype):
        tiles = jnp.concatenate([signed[h][d : d + 1] for h, d in pairs])
        sources = [h * low + d for h, d in pairs]
        return combine(tiles, own, other, sources, first, last, cap, dtype)

    part = sums([(1, d) for d in range(low)], 0, groups, jnp.bfloat16)
    near_sums = swap(part, 2 * low).astype(jnp.float32)
    cut = (groups + 1) // 2
    chunks = {"c": (0, cut), "d": (cut, groups)}
    distant = list(range(2, high))
    arrived = {}
    for key, (first, last) in chunks.items():
        part = sums([(h, d) for d in range(1, low) for h in distant], first, last, jnp.bfloat16)
        part = part.reshape(low - 1, len(distant), -1, LANES)
        arrived[key] = [swap(part[d - 1], 2 * d) for d in range(1, low)]
    kept = sums([(0, d) for d in range(low)] + [(h, 0) for h in distant], 0, groups, jnp.float32)
    combined = kept[0] + near_sums[0]
    for d in range(1, low):
        moved = swap((kept[d] + near_sums[d]).astype(jnp.bfloat16), 2 * d)
        combined = combined + moved.astype(jnp.float32)

    def second(key, i):
        first, last = chunks[key]
        out = kept[low + i, first * GROUP * tokens : last * GROUP * tokens]
        for m in arrived[key]:
            out = out + m[i].astype(jnp.float32)
        return swap(out.astype(jnp.bfloat16), 2 * low * distant[i]).astype(jnp.float32)

    moved = {key: [second(key, i) for i in range(len(distant))] for key in chunks}
    combined = combined + jnp.concatenate([sum(some[1:], some[0]) for some in moved.values()])
    combined = combined.astype(jnp.bfloat16).reshape(tiles, tokens, LANES)
    combined = combined.transpose(1, 0, 2).reshape(tokens, width)

    signed = jnp.concatenate(signed)
    theirs = swap(signed, 1)
    square = squares(own)
    both = statistics(signed, theirs, square, cap)
    bit = 1
    while bit < dp:
        moved = exchange(both, "dp", dp, bit)
        both = both + moved
        bit *= 2
    squared, counts = both[:, 0], both[:, LANES - 1]
    expert_rms = jnp.sqrt(squared / (counts * width) + epsilon)
    counts = counts.astype(jnp.int32)
    return combined, counts, expert_rms


def solution(mesh):
    def step(*args):
        return body(mesh.shape["dp"], mesh.shape["expert"], *args)

    step = jax.shard_map(
        step,
        mesh=mesh,
        in_specs=(
            P("dp", "expert", None, None, None),
            P(("dp", "expert"), None),
            P(("dp", "expert"), None),
        ),
        out_specs=(P(("dp", "expert"), None), P("expert"), P("expert")),
        check_vma=False,
    )
    return step
```

time: 40.9 us -> 42.8 us (1.046)
  waiting for transfers between devices: 10.8 us -> 15 us
  Pallas kernels: 8.44 us -> 6.24 us
    ppermute x10 -> x15, waiting for transfers between devices: 7.12 us -> 15 us  [exchange(): return lax.ppermute(x, axis, [(i, i ^ bit) for i in range(size)])]
    all_to_all x1 -> x0, starting transfers between devices: 7.05 us -> none  [body(): lax.all_to_all(signed, 'expert', split_axis=0, concat_axis=0, tiled=True)]
    ppermute x10 -> x15, starting transfers between devices: 11.3 us -> 18.2 us  [exchange(): return lax.ppermute(x, axis, [(i, i ^ bit) for i in range(size)])]
    all_to_all x1 -> x0, waiting for transfers between devices: 3.65 us -> none  [body(): lax.all_to_all(signed, 'expert', split_axis=0, concat_axis=0, tiled=True)]
    pallas_call x5 -> x7, Pallas kernels: 7.99 us -> 5.8 us  [the longest x4 2.06 us: combine(): pl.pallas_call(functools.partial(combine_kernel, sources=sources, first=f...]
  transfers between devices with their start and end apart: 11 -> 15, of which waited for: 7 -> 7; matrix products, arithmetic and copies ran while one was open for 4% -> 4% of each run, Pallas kernels for 17% -> 14%
where the time goes in v3:
time: 42.8 us; the launch traced here: 42.6 us
  starting transfers between devices  18.2 us (43%)
  waiting for transfers between devices  15 us (35%)
  Pallas kernels  6.24 us (15%)
  other arithmetic  2.3 us (5%)
  between operations  0.78 us (2%)
    ppermute x15, starting transfers between devices, exchange(): return lax.ppermute(x, axis, [(i, i ^ bit) for i in range(size)])  18.2 us
    ppermute x15, waiting for transfers between devices, exchange(): return lax.ppermute(x, axis, [(i, i ^ bit) for i in range(size)])  15 us
    pallas_call x4, Pallas kernels, combine(): pl.pallas_call(functools.partial(combine_kernel, sources=sources, first=f...  2.06 us
    pallas_call x1, Pallas kernels, load(): pl.pallas_call(load_kernel, out_shape=pltpu.VMEM(own.shape, own.dtype), i...  2.05 us
    pallas_call x1, Pallas kernels, squares(): pl.pallas_call(squares_kernel, out_shape=pltpu.VMEM((experts, 8, holders...  0.88 us
  transfers between devices with their start and end apart: 15, of which 7 were waited for; matrix products, arithmetic and copies ran while one was open for 4% of the time, Pallas kernels for 14%

profile of v3, /device:TPU:0, one launch (start us, length us, event | category | flops | bytes accessed | tf_op | source)
XLA Modules:
  0.0 42.6 jit_solution(13565083681150592510)
XLA Ops:
  0.6 0.6 %collective-permute-start.3 = (bf16[8,16,112,128]{3,2,1,0:T(8,128)(2,1)}, bf16[8,16,112,128]{3,2,1,0:T(8,128)(2,1)S(1)}, u32[]{:S(2)}, u32[]{:S(2)}) collective-permute-start(bf16[8,16,112,128]{3,2,1,0:T(8,128)(2,1)} %bitcast.37), channel_id=1, source_target_pairs={{0,1},{1,0},{2,3},{3,2},{4,5},{5,4},{6,7},{7,6},{8,9},{9,8},{10,11... | collective-permute-start | bytes 11010056 | tf_op jit(solution)/shard_map/ppermute | solution.py:220
  1.2 0.8 %weights.1 = f32[8,128]{1,0:T(8,128)S(1)} custom-call(s32[8,8]{1,0:T(8,128)} %ids_hbm.1, f32[8,8]{1,0:T(8,128)} %gates_hbm.1), custom_call_target="tpu_custom_call" | custom-call | tf_op jit(solution)/shard_map/weights/pallas_call | solution.py:69
  2.0 2.6 %collective-permute-start = (f32[8,128]{1,0:T(8,128)S(1)}, f32[8,128]{1,0:T(8,128)S(1)}, u32[]{:S(2)}, u32[]{:S(2)}) collective-permute-start(f32[8,128]{1,0:T(8,128)S(1)} %weights.1), channel_id=1, source_target_pairs={{0,2},{1,3},{2,0},{3,1},{4,6},{5,7},{6,4},{7,5},{8,10},{9,11},{10,... | collective-permute-start | bytes 12296 | tf_op jit(solution)/shard_map/ppermute | solution.py:220
  4.6 2.0 %load.1.own_ref = bf16[8,16,112,128]{3,2,1,0:T(8,128)(2,1)S(1)} custom-call(bf16[8,16,112,128]{3,2,1,0:T(8,128)(2,1)} %bitcast.38), custom_call_target="tpu_custom_call" | custom-call | tf_op jit(solution)/shard_map/load/pallas_call | solution.py:91
  6.7 0.9 %squares.1.squares_ref = f32[8,8,128]{2,1,0:T(8,128)S(1)} custom-call(bf16[8,16,112,128]{3,2,1,0:T(8,128)(2,1)S(1)} %load.1.own_ref), custom_call_target="tpu_custom_call" | custom-call | tf_op jit(solution)/shard_map/squares/pallas_call | solution.py:124
  7.6 1.6 %collective-permute-start.4 = (f32[2,8,128]{2,1,0:T(8,128)S(1)}, f32[2,8,128]{2,1,0:T(8,128)S(1)}, u32[]{:S(2)}, u32[]{:S(2)}) collective-permute-start(f32[2,8,128]{2,1,0:T(8,128)S(1)} %pad_maximum_fusion.1), channel_id=1, source_target_pairs={{0,4},{1,5},{2,6},{3,7},{4,0},{5,1},{6,2},{7,3},{8,12},{9,13},{10,... | collective-permute-start | bytes 24584 | tf_op jit(solution)/shard_map/ppermute | solution.py:220
  9.2 2.5 %collective-permute-start.2 = (f32[2,8,128]{2,1,0:T(8,128)S(1)}, f32[2,8,128]{2,1,0:T(8,128)S(1)}, u32[]{:S(2)}, u32[]{:S(2)}) collective-permute-start(f32[2,8,128]{2,1,0:T(8,128)S(1)} %pad_maximum_fusion.1), channel_id=1, source_target_pairs={{0,12},{1,13},{2,14},{3,15},{4,8},{5,9},{6,10},{7,11},{8,4},{9,5},... | collective-permute-start | bytes 24584 | tf_op jit(solution)/shard_map/ppermute | solution.py:220
  11.8 4.4 %collective-permute-done.1 = f32[2,8,128]{2,1,0:T(8,128)S(1)} collective-permute-done((f32[2,8,128]{2,1,0:T(8,128)S(1)}, f32[2,8,128]{2,1,0:T(8,128)S(1)}, u32[]{:S(2)}, u32[]{:S(2)}) %collective-permute-start.1) | collective-permute-done | bytes 8224 | tf_op jit(solution)/shard_map/ppermute | solution.py:220
  16.3 1.2 %collective-permute-done.13.theirs_ref = f32[8,8,128]{2,1,0:T(8,128)S(1)} collective-permute-done((f32[8,8,128]{2,1,0:T(8,128)S(1)}, f32[8,8,128]{2,1,0:T(8,128)S(1)}, u32[]{:S(2)}, u32[]{:S(2)}) %collective-permute-start.13) | collective-permute-done | bytes 32800 | tf_op jit(solution)/shard_map/ppermute | solution.py:220
  17.9 1.5 %collective-permute-start.14 = (f32[8,128]{1,0:T(8,128)S(1)}, f32[8,128]{1,0:T(8,128)S(1)}, u32[]{:S(2)}, u32[]{:S(2)}) collective-permute-start(f32[8,128]{1,0:T(8,128)S(1)} %statistics.1), channel_id=1, source_target_pairs={{0,16},{16,0},{1,17},{17,1},{2,18},{18,2},{3,19},{19,3},{4,20},{20... | collective-permute-start | bytes 12296 | tf_op jit(solution)/shard_map/ppermute | solution.py:220
  19.4 2.1 %collective-permute-done.14 = f32[8,128]{1,0:T(8,128)S(1)} collective-permute-done((f32[8,128]{1,0:T(8,128)S(1)}, f32[8,128]{1,0:T(8,128)S(1)}, u32[]{:S(2)}, u32[]{:S(2)}) %collective-permute-start.14) | collective-permute-done | bytes 4128 | tf_op jit(solution)/shard_map/ppermute | solution.py:220
  21.6 0.7 %sqrt_reduce_fusion = f32[8]{0:T(128)} fusion(f32[8,128]{1,0:T(8,128)S(1)} %add.56), kind=kLoop, calls=%fused_computation.31 | loop fusion | flops 24 | bytes 96 | tf_op jit(solution)/shard_map/sqrt | solution.py:288
  22.7 0.7 %collective-permute-start.10 = (bf16[2,192,128]{2,1,0:T(8,128)(2,1)S(1)}, bf16[2,192,128]{2,1,0:T(8,128)(2,1)S(1)}, u32[]{:S(2)}, u32[]{:S(2)}) collective-permute-start(bf16[2,192,128]{2,1,0:T(8,128)(2,1)S(1)} %shard_map.61), channel_id=1, source_target_pairs={{0,2},{1,3},{2,0},{3,1},{4,6},{5,7},{6,4},{7,5},{8,10},{9,11},{10,... | collective-permute-start | bytes 294920 | tf_op jit(solution)/shard_map/ppermute | solution.py:220
  23.3 0.7 %convert_reduce_fusion = s32[8]{0:T(128)} fusion(f32[8,128]{1,0:T(8,128)S(1)} %add.56), kind=kLoop, calls=%fused_computation.32 | loop fusion | flops 8 | bytes 64 | tf_op jit(solution)/shard_map/convert_element_type | solution.py:289
  24.4 1.5 %collective-permute-start.7 = (bf16[2,256,128]{2,1,0:T(8,128)(2,1)S(1)}, bf16[2,256,128]{2,1,0:T(8,128)(2,1)S(1)}, u32[]{:S(2)}, u32[]{:S(2)}) collective-permute-start(bf16[2,256,128]{2,1,0:T(8,128)(2,1)S(1)} %shard_map.60), channel_id=1, source_target_pairs={{0,2},{1,3},{2,0},{3,1},{4,6},{5,7},{6,4},{7,5},{8,10},{9,11},{10,... | collective-permute-start | bytes 393224 | tf_op jit(solution)/shard_map/ppermute | solution.py:220
  26.5 0.7 %collective-permute-start.5 = (bf16[2,448,128]{2,1,0:T(8,128)(2,1)S(1)}, bf16[2,448,128]{2,1,0:T(8,128)(2,1)S(1)}, u32[]{:S(2)}, u32[]{:S(2)}) collective-permute-start(bf16[2,448,128]{2,1,0:T(8,128)(2,1)S(1)} %shard_map.59), channel_id=1, source_target_pairs={{0,4},{1,5},{2,6},{3,7},{4,0},{5,1},{6,2},{7,3},{8,12},{9,13},{10,... | collective-permute-start | bytes 688136 | tf_op jit(solution)/shard_map/ppermute | solution.py:220
  27.2 0.8 %shard_map.58 = f32[4,448,128]{2,1,0:T(8,128)S(1)} custom-call(f32[4,8,128]{2,1,0:T(8,128)S(1)} %pad_maximum_fusion.signed_ref, bf16[8,16,112,128]{3,2,1,0:T(8,128)(2,1)S(1)} %load.1.own_ref, bf16[8,16,112,128]{3,2,1,0:T(8,128)(2,1)S(1)} %collective-permute-done.3.other_ref), custom_call_target="tpu_custom_call" | custom-call | tf_op jit(solution)/shard_map/pallas_call | solution.py:210
  28.3 1.0 %collective-permute-start.11 = (bf16[192,128]{1,0:T(8,128)(2,1)S(1)}, bf16[192,128]{1,0:T(8,128)(2,1)S(1)}, u32[]{:S(2)}, u32[]{:S(2)}) collective-permute-start(bf16[192,128]{1,0:T(8,128)(2,1)S(1)} %get-tuple-element.5), channel_id=1, source_target_pairs={{0,8},{1,9},{2,10},{3,11},{4,12},{5,13},{6,14},{7,15},{8,0},{9,1},... | collective-permute-start | bytes 147464 | tf_op jit(solution)/shard_map/ppermute | solution.py:220
  29.3 2.5 %collective-permute-start.12 = (bf16[192,128]{1,0:T(8,128)(2,1)S(1)}, bf16[192,128]{1,0:T(8,128)(2,1)S(1)}, u32[]{:S(2)}, u32[]{:S(2)}) collective-permute-start(bf16[192,128]{1,0:T(8,128)(2,1)S(1)} %get-tuple-element.6), channel_id=1, source_target_pairs={{0,12},{1,13},{2,14},{3,15},{4,8},{5,9},{6,10},{7,11},{8,4},{9,5},... | collective-permute-start | bytes 147464 | tf_op jit(solution)/shard_map/ppermute | solution.py:220
  31.9 2.4 %collective-permute-start.9 = (bf16[256,128]{1,0:T(8,128)(2,1)S(1)}, bf16[256,128]{1,0:T(8,128)(2,1)S(1)}, u32[]{:S(2)}, u32[]{:S(2)}) collective-permute-start(bf16[256,128]{1,0:T(8,128)(2,1)S(1)} %get-tuple-element.4), channel_id=1, source_target_pairs={{0,12},{1,13},{2,14},{3,15},{4,8},{5,9},{6,10},{7,11},{8,4},{9,5},... | collective-permute-start | bytes 196616 | tf_op jit(solution)/shard_map/ppermute | solution.py:220
  34.3 2.5 %collective-permute-done.11 = bf16[192,128]{1,0:T(8,128)(2,1)S(1)} collective-permute-done((bf16[192,128]{1,0:T(8,128)(2,1)S(1)}, bf16[192,128]{1,0:T(8,128)(2,1)S(1)}, u32[]{:S(2)}, u32[]{:S(2)}) %collective-permute-start.11) | collective-permute-done | bytes 49184 | tf_op jit(solution)/shard_map/ppermute | solution.py:220
  37.4 2.4 %collective-permute-done.8 = bf16[256,128]{1,0:T(8,128)(2,1)S(1)} collective-permute-done((bf16[256,128]{1,0:T(8,128)(2,1)S(1)}, bf16[256,128]{1,0:T(8,128)(2,1)S(1)}, u32[]{:S(2)}, u32[]{:S(2)}) %collective-permute-start.8) | collective-permute-done | bytes 65568 | tf_op jit(solution)/shard_map/ppermute | solution.py:220
  39.8 2.1 %collective-permute-done.6 = bf16[448,128]{1,0:T(8,128)(2,1)S(1)} collective-permute-done((bf16[448,128]{1,0:T(8,128)(2,1)S(1)}, bf16[448,128]{1,0:T(8,128)(2,1)S(1)}, u32[]{:S(2)}, u32[]{:S(2)}) %collective-permute-start.6) | collective-permute-done | bytes 114720 | tf_op jit(solution)/shard_map/ppermute | solution.py:220
  41.8 0.7 %fusion.7 = bf16[8,7168]{1,0:T(8,128)(2,1)} fusion(f32[192,128]{1,0:T(8,128)S(1)} %convert_add_fusion.1, f32[256,128]{1,0:T(8,128)S(1)} %convert_add_fusion, bf16[448,128]{1,0:T(8,128)(2,1)S(1)} %collective-permute-done.6, f32[2,448,128]{2,1,0:T(8,128)S(1)} %convert_element_type.73, f32[4,448,128]{2,1,0:T(8,128)S(1)} %shard_map.58), kind=kLoop, calls=%fused_computation.12 | loop fusion | flops 344064 | bytes 917504 | tf_op jit(solution)/shard_map/reshape | solution.py:276
  (34 shorter events, 2.9 us)
Async XLA Ops:
  0.6 21.7 %collective-permute-start.3 = (bf16[8,16,112,128]{3,2,1,0:T(8,128)(2,1)}, bf16[8,16,112,128]{3,2,1,0:T(8,128)(2,1)S(1)}, u32[]{:S(2)}, u32[]{:S(2)}) collective-permute-start(bf16[8,16,112,128]{3,2,1,0:T(8,128)(2,1)} %bitcast.37), channel_id=1, source_target_pairs={{0,1},{1,0},{2,3},{3,2},{4,5},{5,4},{6,7},{7,6},{8,9},{9,8},{10,11... | collective-permute-start | bytes 11010056 | tf_op jit(solution)/shard_map/ppermute | solution.py:220
  2.0 5.5 %collective-permute-start = (f32[8,128]{1,0:T(8,128)S(1)}, f32[8,128]{1,0:T(8,128)S(1)}, u32[]{:S(2)}, u32[]{:S(2)}) collective-permute-start(f32[8,128]{1,0:T(8,128)S(1)} %weights.1), channel_id=1, source_target_pairs={{0,2},{1,3},{2,0},{3,1},{4,6},{5,7},{6,4},{7,5},{8,10},{9,11},{10,... | collective-permute-start | bytes 12296 | tf_op jit(solution)/shard_map/ppermute | solution.py:220
  7.6 4.2 %collective-permute-start.4 = (f32[2,8,128]{2,1,0:T(8,128)S(1)}, f32[2,8,128]{2,1,0:T(8,128)S(1)}, u32[]{:S(2)}, u32[]{:S(2)}) collective-permute-start(f32[2,8,128]{2,1,0:T(8,128)S(1)} %pad_maximum_fusion.1), channel_id=1, source_target_pairs={{0,4},{1,5},{2,6},{3,7},{4,0},{5,1},{6,2},{7,3},{8,12},{9,13},{10,... | collective-permute-start | bytes 24584 | tf_op jit(solution)/shard_map/ppermute | solution.py:220
  9.2 7.0 %collective-permute-start.2 = (f32[2,8,128]{2,1,0:T(8,128)S(1)}, f32[2,8,128]{2,1,0:T(8,128)S(1)}, u32[]{:S(2)}, u32[]{:S(2)}) collective-permute-start(f32[2,8,128]{2,1,0:T(8,128)S(1)} %pad_maximum_fusion.1), channel_id=1, source_target_pairs={{0,12},{1,13},{2,14},{3,15},{4,8},{5,9},{6,10},{7,11},{8,4},{9,5},... | collective-permute-start | bytes 24584 | tf_op jit(solution)/shard_map/ppermute | solution.py:220
  11.7 4.5 %collective-permute-start.1 = (f32[2,8,128]{2,1,0:T(8,128)S(1)}, f32[2,8,128]{2,1,0:T(8,128)S(1)}, u32[]{:S(2)}, u32[]{:S(2)}) collective-permute-start(f32[2,8,128]{2,1,0:T(8,128)S(1)} %pad_maximum_fusion.1), channel_id=1, source_target_pairs={{0,8},{1,9},{2,10},{3,11},{4,12},{5,13},{6,14},{7,15},{8,0},{9,1},... | collective-permute-start | bytes 24584 | tf_op jit(solution)/shard_map/ppermute | solution.py:220
  16.2 1.3 %collective-permute-start.13 = (f32[8,8,128]{2,1,0:T(8,128)S(1)}, f32[8,8,128]{2,1,0:T(8,128)S(1)}, u32[]{:S(2)}, u32[]{:S(2)}) collective-permute-start(f32[8,8,128]{2,1,0:T(8,128)S(1)} %constant_dynamic-update-slice_fusion.mine_ref), channel_id=1, source_target_pairs={{0,1},{1,0},{2,3},{3,2},{4,5},{5,4},{6,7},{7,6},{8,9},{9,8},{10,11... | collective-permute-start | bytes 98312 | tf_op jit(solution)/shard_map/ppermute | solution.py:220
  17.9 3.6 %collective-permute-start.14 = (f32[8,128]{1,0:T(8,128)S(1)}, f32[8,128]{1,0:T(8,128)S(1)}, u32[]{:S(2)}, u32[]{:S(2)}) collective-permute-start(f32[8,128]{1,0:T(8,128)S(1)} %statistics.1), channel_id=1, source_target_pairs={{0,16},{16,0},{1,17},{17,1},{2,18},{18,2},{3,19},{19,3},{4,20},{20... | collective-permute-start | bytes 12296 | tf_op jit(solution)/shard_map/ppermute | solution.py:220
  22.7 5.6 %collective-permute-start.10 = (bf16[2,192,128]{2,1,0:T(8,128)(2,1)S(1)}, bf16[2,192,128]{2,1,0:T(8,128)(2,1)S(1)}, u32[]{:S(2)}, u32[]{:S(2)}) collective-permute-start(bf16[2,192,128]{2,1,0:T(8,128)(2,1)S(1)} %shard_map.61), channel_id=1, source_target_pairs={{0,2},{1,3},{2,0},{3,1},{4,6},{5,7},{6,4},{7,5},{8,10},{9,11},{10,... | collective-permute-start | bytes 294920 | tf_op jit(solution)/shard_map/ppermute | solution.py:220
  24.4 7.4 %collective-permute-start.7 = (bf16[2,256,128]{2,1,0:T(8,128)(2,1)S(1)}, bf16[2,256,128]{2,1,0:T(8,128)(2,1)S(1)}, u32[]{:S(2)}, u32[]{:S(2)}) collective-permute-start(bf16[2,256,128]{2,1,0:T(8,128)(2,1)S(1)} %shard_map.60), channel_id=1, source_target_pairs={{0,2},{1,3},{2,0},{3,1},{4,6},{5,7},{6,4},{7,5},{8,10},{9,11},{10,... | collective-permute-start | bytes 393224 | tf_op jit(solution)/shard_map/ppermute | solution.py:220
  26.5 10.4 %collective-permute-start.5 = (bf16[2,448,128]{2,1,0:T(8,128)(2,1)S(1)}, bf16[2,448,128]{2,1,0:T(8,128)(2,1)S(1)}, u32[]{:S(2)}, u32[]{:S(2)}) collective-permute-start(bf16[2,448,128]{2,1,0:T(8,128)(2,1)S(1)} %shard_map.59), channel_id=1, source_target_pairs={{0,4},{1,5},{2,6},{3,7},{4,0},{5,1},{6,2},{7,3},{8,12},{9,13},{10,... | collective-permute-start | bytes 688136 | tf_op jit(solution)/shard_map/ppermute | solution.py:220
  28.3 8.6 %collective-permute-start.11 = (bf16[192,128]{1,0:T(8,128)(2,1)S(1)}, bf16[192,128]{1,0:T(8,128)(2,1)S(1)}, u32[]{:S(2)}, u32[]{:S(2)}) collective-permute-start(bf16[192,128]{1,0:T(8,128)(2,1)S(1)} %get-tuple-element.5), channel_id=1, source_target_pairs={{0,8},{1,9},{2,10},{3,11},{4,12},{5,13},{6,14},{7,15},{8,0},{9,1},... | collective-permute-start | bytes 147464 | tf_op jit(solution)/shard_map/ppermute | solution.py:220
  29.3 7.6 %collective-permute-start.12 = (bf16[192,128]{1,0:T(8,128)(2,1)S(1)}, bf16[192,128]{1,0:T(8,128)(2,1)S(1)}, u32[]{:S(2)}, u32[]{:S(2)}) collective-permute-start(bf16[192,128]{1,0:T(8,128)(2,1)S(1)} %get-tuple-element.6), channel_id=1, source_target_pairs={{0,12},{1,13},{2,14},{3,15},{4,8},{5,9},{6,10},{7,11},{8,4},{9,5},... | collective-permute-start | bytes 147464 | tf_op jit(solution)/shard_map/ppermute | solution.py:220
  31.8 7.9 %collective-permute-start.8 = (bf16[256,128]{1,0:T(8,128)(2,1)S(1)}, bf16[256,128]{1,0:T(8,128)(2,1)S(1)}, u32[]{:S(2)}, u32[]{:S(2)}) collective-permute-start(bf16[256,128]{1,0:T(8,128)(2,1)S(1)} %get-tuple-element.3), channel_id=1, source_target_pairs={{0,8},{1,9},{2,10},{3,11},{4,12},{5,13},{6,14},{7,15},{8,0},{9,1},... | collective-permute-start | bytes 196616 | tf_op jit(solution)/shard_map/ppermute | solution.py:220
  31.9 7.9 %collective-permute-start.9 = (bf16[256,128]{1,0:T(8,128)(2,1)S(1)}, bf16[256,128]{1,0:T(8,128)(2,1)S(1)}, u32[]{:S(2)}, u32[]{:S(2)}) collective-permute-start(bf16[256,128]{1,0:T(8,128)(2,1)S(1)} %get-tuple-element.4), channel_id=1, source_target_pairs={{0,12},{1,13},{2,14},{3,15},{4,8},{5,9},{6,10},{7,11},{8,4},{9,5},... | collective-permute-start | bytes 196616 | tf_op jit(solution)/shard_map/ppermute | solution.py:220
  37.0 4.9 %collective-permute-start.6 = (bf16[448,128]{1,0:T(8,128)(2,1)S(1)}, bf16[448,128]{1,0:T(8,128)(2,1)S(1)}, u32[]{:S(2)}, u32[]{:S(2)}) collective-permute-start(bf16[448,128]{1,0:T(8,128)(2,1)S(1)} %fusion.8), channel_id=1, source_target_pairs={{0,2},{1,3},{2,0},{3,1},{4,6},{5,7},{6,4},{7,5},{8,10},{9,11},{10,... | collective-permute-start | bytes 344072 | tf_op jit(solution)/shard_map/ppermute | solution.py:220

commit v4 on v3

--- a/solution.py
+++ b/solution.py
@@ -155,15 +155,21 @@
     square = jnp.zeros((experts, wide), jnp.float32)
     for e in range(experts):
         square = jnp.where(row == e, jnp.broadcast_to(squares_ref[e, 0:1, :], square.shape), square)
-    sums = jnp.sum(total * square, axis=1, keepdims=True)
-    counts = jnp.sum(total, axis=1, keepdims=True) * (cap / 8)
-    out_ref[...] = jnp.where(iota(out_ref.shape, 1) < LANES // 2, sums, counts)
+    ones = jnp.ones((8, wide), jnp.float32)
+    sums, counts = [
+        lax.dot_general(
+            ones, x, (((1,), (1,)), ((), ())),
+            precision=lax.Precision.HIGHEST, preferred_element_type=jnp.float32,
+        )
+        for x in (total * square, total * (cap / 8))
+    ]
+    out_ref[...] = jnp.where(iota(out_ref.shape, 0) == 0, sums, counts)
 
 
 def statistics(mine, theirs, square, cap):
     return pl.pallas_call(
         functools.partial(statistics_kernel, cap=cap),
-        out_shape=pltpu.VMEM((square.shape[0], LANES), jnp.float32),
+        out_shape=pltpu.VMEM((8, square.shape[0]), jnp.float32),
         in_specs=[VMEM, VMEM, VMEM],
         out_specs=VMEM,
         compiler_params=params(),
@@ -249,7 +255,7 @@
 
     part = sums([(1, d) for d in range(low)], 0, groups, jnp.bfloat16)
     near_sums = swap(part, 2 * low).astype(jnp.float32)
-    cut = (groups + 1) // 2
+    cut = groups // 2
     chunks = {"c": (0, cut), "d": (cut, groups)}
     distant = list(range(2, high))
     arrived = {}
@@ -284,7 +290,7 @@
         moved = exchange(both, "dp", dp, bit)
         both = both + moved
         bit *= 2
-    squared, counts = both[:, 0], both[:, LANES - 1]
+    squared, counts = both[0], both[1]
     expert_rms = jnp.sqrt(squared / (counts * width) + epsilon)
     counts = counts.astype(jnp.int32)
     return combined, counts, expert_rms

time: 42.8 us -> 42 us (0.981)
  other arithmetic: 2.3 us -> 1.42 us
    convert_element_type x1 -> x0, other arithmetic: 0.69 us -> none  [body(): counts = counts.astype(jnp.int32)]
  transfers between devices with their start and end apart: 15 -> 15, of which waited for: 7 -> 7; matrix products, arithmetic and copies ran while one was open for 4% -> 2% of each run, Pallas kernels for 14% -> 14%
where the time goes in v4:
time: 42 us; the launch traced here: 41.7 us
  starting transfers between devices  18.5 us (44%)
  waiting for transfers between devices  14.7 us (35%)
  Pallas kernels  6.3 us (15%)
  other arithmetic  1.42 us (3%)
  between operations  0.78 us (2%)
    ppermute x15, starting transfers between devices, exchange(): return lax.ppermute(x, axis, [(i, i ^ bit) for i in range(size)])  18.5 us
    ppermute x15, waiting for transfers between devices, exchange(): return lax.ppermute(x, axis, [(i, i ^ bit) for i in range(size)])  14.7 us
    pallas_call x4, Pallas kernels, combine(): pl.pallas_call(functools.partial(combine_kernel, sources=sources, first=f...  2.07 us
    pallas_call x1, Pallas kernels, load(): pl.pallas_call(load_kernel, out_shape=pltpu.VMEM(own.shape, own.dtype), i...  2.05 us
    pallas_call x1, Pallas kernels, squares(): pl.pallas_call(squares_kernel, out_shape=pltpu.VMEM((experts, 8, holders...  0.88 us
  transfers between devices with their start and end apart: 15, of which 7 were waited for; matrix products, arithmetic and copies ran while one was open for 2% of the time, Pallas kernels for 14%

profile of v4, /device:TPU:0, one launch (start us, length us, event | category | flops | bytes accessed | tf_op | source)
XLA Modules:
  0.0 41.7 jit_solution(16822267797772402283)
XLA Ops:
  0.6 0.6 %collective-permute-start.3 = (bf16[8,16,112,128]{3,2,1,0:T(8,128)(2,1)}, bf16[8,16,112,128]{3,2,1,0:T(8,128)(2,1)S(1)}, u32[]{:S(2)}, u32[]{:S(2)}) collective-permute-start(bf16[8,16,112,128]{3,2,1,0:T(8,128)(2,1)} %bitcast.41), channel_id=1, source_target_pairs={{0,1},{1,0},{2,3},{3,2},{4,5},{5,4},{6,7},{7,6},{8,9},{9,8},{10,11... | collective-permute-start | bytes 11010056 | tf_op jit(solution)/shard_map/ppermute | solution.py:226
  1.2 0.8 %weights.1 = f32[8,128]{1,0:T(8,128)S(1)} custom-call(s32[8,8]{1,0:T(8,128)} %ids_hbm.1, f32[8,8]{1,0:T(8,128)} %gates_hbm.1), custom_call_target="tpu_custom_call" | custom-call | tf_op jit(solution)/shard_map/weights/pallas_call | solution.py:69
  2.0 2.6 %collective-permute-start = (f32[8,128]{1,0:T(8,128)S(1)}, f32[8,128]{1,0:T(8,128)S(1)}, u32[]{:S(2)}, u32[]{:S(2)}) collective-permute-start(f32[8,128]{1,0:T(8,128)S(1)} %weights.1), channel_id=1, source_target_pairs={{0,2},{1,3},{2,0},{3,1},{4,6},{5,7},{6,4},{7,5},{8,10},{9,11},{10,... | collective-permute-start | bytes 12296 | tf_op jit(solution)/shard_map/ppermute | solution.py:226
  4.6 2.0 %load.1.own_ref = bf16[8,16,112,128]{3,2,1,0:T(8,128)(2,1)S(1)} custom-call(bf16[8,16,112,128]{3,2,1,0:T(8,128)(2,1)} %bitcast.42), custom_call_target="tpu_custom_call" | custom-call | tf_op jit(solution)/shard_map/load/pallas_call | solution.py:91
  6.7 0.9 %squares.1.squares_ref = f32[8,8,128]{2,1,0:T(8,128)S(1)} custom-call(bf16[8,16,112,128]{3,2,1,0:T(8,128)(2,1)S(1)} %load.1.own_ref), custom_call_target="tpu_custom_call" | custom-call | tf_op jit(solution)/shard_map/squares/pallas_call | solution.py:124
  7.6 1.6 %collective-permute-start.4 = (f32[2,8,128]{2,1,0:T(8,128)S(1)}, f32[2,8,128]{2,1,0:T(8,128)S(1)}, u32[]{:S(2)}, u32[]{:S(2)}) collective-permute-start(f32[2,8,128]{2,1,0:T(8,128)S(1)} %pad_maximum_fusion.1), channel_id=1, source_target_pairs={{0,4},{1,5},{2,6},{3,7},{4,0},{5,1},{6,2},{7,3},{8,12},{9,13},{10,... | collective-permute-start | bytes 24584 | tf_op jit(solution)/shard_map/ppermute | solution.py:226
  9.2 2.5 %collective-permute-start.2 = (f32[2,8,128]{2,1,0:T(8,128)S(1)}, f32[2,8,128]{2,1,0:T(8,128)S(1)}, u32[]{:S(2)}, u32[]{:S(2)}) collective-permute-start(f32[2,8,128]{2,1,0:T(8,128)S(1)} %pad_maximum_fusion.1), channel_id=1, source_target_pairs={{0,12},{1,13},{2,14},{3,15},{4,8},{5,9},{6,10},{7,11},{8,4},{9,5},... | collective-permute-start | bytes 24584 | tf_op jit(solution)/shard_map/ppermute | solution.py:226
  11.8 4.4 %collective-permute-done.1 = f32[2,8,128]{2,1,0:T(8,128)S(1)} collective-permute-done((f32[2,8,128]{2,1,0:T(8,128)S(1)}, f32[2,8,128]{2,1,0:T(8,128)S(1)}, u32[]{:S(2)}, u32[]{:S(2)}) %collective-permute-start.1) | collective-permute-done | bytes 8224 | tf_op jit(solution)/shard_map/ppermute | solution.py:226
  16.3 1.2 %collective-permute-done.13.theirs_ref = f32[8,8,128]{2,1,0:T(8,128)S(1)} collective-permute-done((f32[8,8,128]{2,1,0:T(8,128)S(1)}, f32[8,8,128]{2,1,0:T(8,128)S(1)}, u32[]{:S(2)}, u32[]{:S(2)}) %collective-permute-start.13) | collective-permute-done | bytes 32800 | tf_op jit(solution)/shard_map/ppermute | solution.py:226
  18.0 1.5 %collective-permute-start.14 = (f32[8,8]{1,0:T(8,128)S(1)}, f32[8,8]{1,0:T(8,128)S(1)}, u32[]{:S(2)}, u32[]{:S(2)}) collective-permute-start(f32[8,8]{1,0:T(8,128)S(1)} %statistics.1), channel_id=1, source_target_pairs={{0,16},{16,0},{1,17},{17,1},{2,18},{18,2},{3,19},{19,3},{4,20},{20... | collective-permute-start | bytes 776 | tf_op jit(solution)/shard_map/ppermute | solution.py:226
  19.5 2.1 %collective-permute-done.14 = f32[8,8]{1,0:T(8,128)S(1)} collective-permute-done((f32[8,8]{1,0:T(8,128)S(1)}, f32[8,8]{1,0:T(8,128)S(1)}, u32[]{:S(2)}, u32[]{:S(2)}) %collective-permute-start.14) | collective-permute-done | bytes 288 | tf_op jit(solution)/shard_map/ppermute | solution.py:226
  22.0 0.6 %collective-permute-start.7 = (bf16[2,192,128]{2,1,0:T(8,128)(2,1)S(1)}, bf16[2,192,128]{2,1,0:T(8,128)(2,1)S(1)}, u32[]{:S(2)}, u32[]{:S(2)}) collective-permute-start(bf16[2,192,128]{2,1,0:T(8,128)(2,1)S(1)} %shard_map.60), channel_id=1, source_target_pairs={{0,2},{1,3},{2,0},{3,1},{4,6},{5,7},{6,4},{7,5},{8,10},{9,11},{10,... | collective-permute-start | bytes 294920 | tf_op jit(solution)/shard_map/ppermute | solution.py:226
  22.7 0.5 %sqrt_bitcast_fusion = (f32[8]{0:T(128)}, s32[8]{0:T(128)}) fusion(f32[8,8]{1,0:T(8,128)S(1)} %add.56), kind=kLoop, calls=%fused_computation.31 | loop fusion | flops 32 | bytes 128 | tf_op jit(solution)/shard_map/sqrt | solution.py:294
  23.6 1.5 %collective-permute-start.10 = (bf16[2,256,128]{2,1,0:T(8,128)(2,1)S(1)}, bf16[2,256,128]{2,1,0:T(8,128)(2,1)S(1)}, u32[]{:S(2)}, u32[]{:S(2)}) collective-permute-start(bf16[2,256,128]{2,1,0:T(8,128)(2,1)S(1)} %shard_map.61), channel_id=1, source_target_pairs={{0,2},{1,3},{2,0},{3,1},{4,6},{5,7},{6,4},{7,5},{8,10},{9,11},{10,... | collective-permute-start | bytes 393224 | tf_op jit(solution)/shard_map/ppermute | solution.py:226
  25.7 0.7 %collective-permute-start.5 = (bf16[2,448,128]{2,1,0:T(8,128)(2,1)S(1)}, bf16[2,448,128]{2,1,0:T(8,128)(2,1)S(1)}, u32[]{:S(2)}, u32[]{:S(2)}) collective-permute-start(bf16[2,448,128]{2,1,0:T(8,128)(2,1)S(1)} %shard_map.59), channel_id=1, source_target_pairs={{0,4},{1,5},{2,6},{3,7},{4,0},{5,1},{6,2},{7,3},{8,12},{9,13},{10,... | collective-permute-start | bytes 688136 | tf_op jit(solution)/shard_map/ppermute | solution.py:226
  26.4 0.8 %shard_map.58 = f32[4,448,128]{2,1,0:T(8,128)S(1)} custom-call(f32[4,8,128]{2,1,0:T(8,128)S(1)} %pad_maximum_fusion.signed_ref, bf16[8,16,112,128]{3,2,1,0:T(8,128)(2,1)S(1)} %load.1.own_ref, bf16[8,16,112,128]{3,2,1,0:T(8,128)(2,1)S(1)} %collective-permute-done.3.other_ref), custom_call_target="tpu_custom_call" | custom-call | tf_op jit(solution)/shard_map/pallas_call | solution.py:216
  27.5 1.0 %collective-permute-start.8 = (bf16[192,128]{1,0:T(8,128)(2,1)S(1)}, bf16[192,128]{1,0:T(8,128)(2,1)S(1)}, u32[]{:S(2)}, u32[]{:S(2)}) collective-permute-start(bf16[192,128]{1,0:T(8,128)(2,1)S(1)} %get-tuple-element.5), channel_id=1, source_target_pairs={{0,8},{1,9},{2,10},{3,11},{4,12},{5,13},{6,14},{7,15},{8,0},{9,1},... | collective-permute-start | bytes 147464 | tf_op jit(solution)/shard_map/ppermute | solution.py:226
  28.5 2.5 %collective-permute-start.9 = (bf16[192,128]{1,0:T(8,128)(2,1)S(1)}, bf16[192,128]{1,0:T(8,128)(2,1)S(1)}, u32[]{:S(2)}, u32[]{:S(2)}) collective-permute-start(bf16[192,128]{1,0:T(8,128)(2,1)S(1)} %get-tuple-element.6), channel_id=1, source_target_pairs={{0,12},{1,13},{2,14},{3,15},{4,8},{5,9},{6,10},{7,11},{8,4},{9,5},... | collective-permute-start | bytes 147464 | tf_op jit(solution)/shard_map/ppermute | solution.py:226
  31.1 2.4 %collective-permute-start.12 = (bf16[256,128]{1,0:T(8,128)(2,1)S(1)}, bf16[256,128]{1,0:T(8,128)(2,1)S(1)}, u32[]{:S(2)}, u32[]{:S(2)}) collective-permute-start(bf16[256,128]{1,0:T(8,128)(2,1)S(1)} %get-tuple-element.4), channel_id=1, source_target_pairs={{0,12},{1,13},{2,14},{3,15},{4,8},{5,9},{6,10},{7,11},{8,4},{9,5},... | collective-permute-start | bytes 196616 | tf_op jit(solution)/shard_map/ppermute | solution.py:226
  33.5 2.5 %collective-permute-done.8 = bf16[192,128]{1,0:T(8,128)(2,1)S(1)} collective-permute-done((bf16[192,128]{1,0:T(8,128)(2,1)S(1)}, bf16[192,128]{1,0:T(8,128)(2,1)S(1)}, u32[]{:S(2)}, u32[]{:S(2)}) %collective-permute-start.8) | collective-permute-done | bytes 49184 | tf_op jit(solution)/shard_map/ppermute | solution.py:226
  36.2 0.7 %collective-permute-start.6 = (bf16[448,128]{1,0:T(8,128)(2,1)S(1)}, bf16[448,128]{1,0:T(8,128)(2,1)S(1)}, u32[]{:S(2)}, u32[]{:S(2)}) collective-permute-start(bf16[448,128]{1,0:T(8,128)(2,1)S(1)} %fusion.8), channel_id=1, source_target_pairs={{0,2},{1,3},{2,0},{3,1},{4,6},{5,7},{6,4},{7,5},{8,10},{9,11},{10,... | collective-permute-start | bytes 344072 | tf_op jit(solution)/shard_map/ppermute | solution.py:226
  36.9 2.1 %collective-permute-done.11 = bf16[256,128]{1,0:T(8,128)(2,1)S(1)} collective-permute-done((bf16[256,128]{1,0:T(8,128)(2,1)S(1)}, bf16[256,128]{1,0:T(8,128)(2,1)S(1)}, u32[]{:S(2)}, u32[]{:S(2)}) %collective-permute-start.11) | collective-permute-done | bytes 65568 | tf_op jit(solution)/shard_map/ppermute | solution.py:226
  39.0 2.0 %collective-permute-done.6 = bf16[448,128]{1,0:T(8,128)(2,1)S(1)} collective-permute-done((bf16[448,128]{1,0:T(8,128)(2,1)S(1)}, bf16[448,128]{1,0:T(8,128)(2,1)S(1)}, u32[]{:S(2)}, u32[]{:S(2)}) %collective-permute-start.6) | collective-permute-done | bytes 114720 | tf_op jit(solution)/shard_map/ppermute | solution.py:226
  41.0 0.7 %fusion.7 = bf16[8,7168]{1,0:T(8,128)(2,1)} fusion(f32[256,128]{1,0:T(8,128)S(1)} %convert_add_fusion, f32[192,128]{1,0:T(8,128)S(1)} %convert_add_fusion.1, bf16[448,128]{1,0:T(8,128)(2,1)S(1)} %collective-permute-done.6, f32[2,448,128]{2,1,0:T(8,128)S(1)} %convert_element_type.73, f32[4,448,128]{2,1,0:T(8,128)S(1)} %shard_map.58), kind=kLoop, calls=%fused_computation.12 | loop fusion | flops 344064 | bytes 917504 | tf_op jit(solution)/shard_map/reshape | solution.py:282
  (33 shorter events, 2.6 us)
Async XLA Ops:
  0.6 21.0 %collective-permute-start.3 = (bf16[8,16,112,128]{3,2,1,0:T(8,128)(2,1)}, bf16[8,16,112,128]{3,2,1,0:T(8,128)(2,1)S(1)}, u32[]{:S(2)}, u32[]{:S(2)}) collective-permute-start(bf16[8,16,112,128]{3,2,1,0:T(8,128)(2,1)} %bitcast.41), channel_id=1, source_target_pairs={{0,1},{1,0},{2,3},{3,2},{4,5},{5,4},{6,7},{7,6},{8,9},{9,8},{10,11... | collective-permute-start | bytes 11010056 | tf_op jit(solution)/shard_map/ppermute | solution.py:226
  2.0 5.5 %collective-permute-start = (f32[8,128]{1,0:T(8,128)S(1)}, f32[8,128]{1,0:T(8,128)S(1)}, u32[]{:S(2)}, u32[]{:S(2)}) collective-permute-start(f32[8,128]{1,0:T(8,128)S(1)} %weights.1), channel_id=1, source_target_pairs={{0,2},{1,3},{2,0},{3,1},{4,6},{5,7},{6,4},{7,5},{8,10},{9,11},{10,... | collective-permute-start | bytes 12296 | tf_op jit(solution)/shard_map/ppermute | solution.py:226
  7.6 4.2 %collective-permute-start.4 = (f32[2,8,128]{2,1,0:T(8,128)S(1)}, f32[2,8,128]{2,1,0:T(8,128)S(1)}, u32[]{:S(2)}, u32[]{:S(2)}) collective-permute-start(f32[2,8,128]{2,1,0:T(8,128)S(1)} %pad_maximum_fusion.1), channel_id=1, source_target_pairs={{0,4},{1,5},{2,6},{3,7},{4,0},{5,1},{6,2},{7,3},{8,12},{9,13},{10,... | collective-permute-start | bytes 24584 | tf_op jit(solution)/shard_map/ppermute | solution.py:226
  9.2 7.0 %collective-permute-start.2 = (f32[2,8,128]{2,1,0:T(8,128)S(1)}, f32[2,8,128]{2,1,0:T(8,128)S(1)}, u32[]{:S(2)}, u32[]{:S(2)}) collective-permute-start(f32[2,8,128]{2,1,0:T(8,128)S(1)} %pad_maximum_fusion.1), channel_id=1, source_target_pairs={{0,12},{1,13},{2,14},{3,15},{4,8},{5,9},{6,10},{7,11},{8,4},{9,5},... | collective-permute-start | bytes 24584 | tf_op jit(solution)/shard_map/ppermute | solution.py:226
  11.7 4.5 %collective-permute-start.1 = (f32[2,8,128]{2,1,0:T(8,128)S(1)}, f32[2,8,128]{2,1,0:T(8,128)S(1)}, u32[]{:S(2)}, u32[]{:S(2)}) collective-permute-start(f32[2,8,128]{2,1,0:T(8,128)S(1)} %pad_maximum_fusion.1), channel_id=1, source_target_pairs={{0,8},{1,9},{2,10},{3,11},{4,12},{5,13},{6,14},{7,15},{8,0},{9,1},... | collective-permute-start | bytes 24584 | tf_op jit(solution)/shard_map/ppermute | solution.py:226
  16.2 1.3 %collective-permute-start.13 = (f32[8,8,128]{2,1,0:T(8,128)S(1)}, f32[8,8,128]{2,1,0:T(8,128)S(1)}, u32[]{:S(2)}, u32[]{:S(2)}) collective-permute-start(f32[8,8,128]{2,1,0:T(8,128)S(1)} %constant_dynamic-update-slice_fusion.mine_ref), channel_id=1, source_target_pairs={{0,1},{1,0},{2,3},{3,2},{4,5},{5,4},{6,7},{7,6},{8,9},{9,8},{10,11... | collective-permute-start | bytes 98312 | tf_op jit(solution)/shard_map/ppermute | solution.py:226
  18.0 3.6 %collective-permute-start.14 = (f32[8,8]{1,0:T(8,128)S(1)}, f32[8,8]{1,0:T(8,128)S(1)}, u32[]{:S(2)}, u32[]{:S(2)}) collective-permute-start(f32[8,8]{1,0:T(8,128)S(1)} %statistics.1), channel_id=1, source_target_pairs={{0,16},{16,0},{1,17},{17,1},{2,18},{18,2},{3,19},{19,3},{4,20},{20... | collective-permute-start | bytes 776 | tf_op jit(solution)/shard_map/ppermute | solution.py:226
  22.0 5.5 %collective-permute-start.7 = (bf16[2,192,128]{2,1,0:T(8,128)(2,1)S(1)}, bf16[2,192,128]{2,1,0:T(8,128)(2,1)S(1)}, u32[]{:S(2)}, u32[]{:S(2)}) collective-permute-start(bf16[2,192,128]{2,1,0:T(8,128)(2,1)S(1)} %shard_map.60), channel_id=1, source_target_pairs={{0,2},{1,3},{2,0},{3,1},{4,6},{5,7},{6,4},{7,5},{8,10},{9,11},{10,... | collective-permute-start | bytes 294920 | tf_op jit(solution)/shard_map/ppermute | solution.py:226
  23.6 7.4 %collective-permute-start.10 = (bf16[2,256,128]{2,1,0:T(8,128)(2,1)S(1)}, bf16[2,256,128]{2,1,0:T(8,128)(2,1)S(1)}, u32[]{:S(2)}, u32[]{:S(2)}) collective-permute-start(bf16[2,256,128]{2,1,0:T(8,128)(2,1)S(1)} %shard_map.61), channel_id=1, source_target_pairs={{0,2},{1,3},{2,0},{3,1},{4,6},{5,7},{6,4},{7,5},{8,10},{9,11},{10,... | collective-permute-start | bytes 393224 | tf_op jit(solution)/shard_map/ppermute | solution.py:226
  25.7 10.4 %collective-permute-start.5 = (bf16[2,448,128]{2,1,0:T(8,128)(2,1)S(1)}, bf16[2,448,128]{2,1,0:T(8,128)(2,1)S(1)}, u32[]{:S(2)}, u32[]{:S(2)}) collective-permute-start(bf16[2,448,128]{2,1,0:T(8,128)(2,1)S(1)} %shard_map.59), channel_id=1, source_target_pairs={{0,4},{1,5},{2,6},{3,7},{4,0},{5,1},{6,2},{7,3},{8,12},{9,13},{10,... | collective-permute-start | bytes 688136 | tf_op jit(solution)/shard_map/ppermute | solution.py:226
  27.5 8.6 %collective-permute-start.8 = (bf16[192,128]{1,0:T(8,128)(2,1)S(1)}, bf16[192,128]{1,0:T(8,128)(2,1)S(1)}, u32[]{:S(2)}, u32[]{:S(2)}) collective-permute-start(bf16[192,128]{1,0:T(8,128)(2,1)S(1)} %get-tuple-element.5), channel_id=1, source_target_pairs={{0,8},{1,9},{2,10},{3,11},{4,12},{5,13},{6,14},{7,15},{8,0},{9,1},... | collective-permute-start | bytes 147464 | tf_op jit(solution)/shard_map/ppermute | solution.py:226
  28.5 7.6 %collective-permute-start.9 = (bf16[192,128]{1,0:T(8,128)(2,1)S(1)}, bf16[192,128]{1,0:T(8,128)(2,1)S(1)}, u32[]{:S(2)}, u32[]{:S(2)}) collective-permute-start(bf16[192,128]{1,0:T(8,128)(2,1)S(1)} %get-tuple-element.6), channel_id=1, source_target_pairs={{0,12},{1,13},{2,14},{3,15},{4,8},{5,9},{6,10},{7,11},{8,4},{9,5},... | collective-permute-start | bytes 147464 | tf_op jit(solution)/shard_map/ppermute | solution.py:226
  31.0 7.9 %collective-permute-start.11 = (bf16[256,128]{1,0:T(8,128)(2,1)S(1)}, bf16[256,128]{1,0:T(8,128)(2,1)S(1)}, u32[]{:S(2)}, u32[]{:S(2)}) collective-permute-start(bf16[256,128]{1,0:T(8,128)(2,1)S(1)} %get-tuple-element.3), channel_id=1, source_target_pairs={{0,8},{1,9},{2,10},{3,11},{4,12},{5,13},{6,14},{7,15},{8,0},{9,1},... | collective-permute-start | bytes 196616 | tf_op jit(solution)/shard_map/ppermute | solution.py:226
  31.1 7.9 %collective-permute-start.12 = (bf16[256,128]{1,0:T(8,128)(2,1)S(1)}, bf16[256,128]{1,0:T(8,128)(2,1)S(1)}, u32[]{:S(2)}, u32[]{:S(2)}) collective-permute-start(bf16[256,128]{1,0:T(8,128)(2,1)S(1)} %get-tuple-element.4), channel_id=1, source_target_pairs={{0,12},{1,13},{2,14},{3,15},{4,8},{5,9},{6,10},{7,11},{8,4},{9,5},... | collective-permute-start | bytes 196616 | tf_op jit(solution)/shard_map/ppermute | solution.py:226
  36.2 4.9 %collective-permute-start.6 = (bf16[448,128]{1,0:T(8,128)(2,1)S(1)}, bf16[448,128]{1,0:T(8,128)(2,1)S(1)}, u32[]{:S(2)}, u32[]{:S(2)}) collective-permute-start(bf16[448,128]{1,0:T(8,128)(2,1)S(1)} %fusion.8), channel_id=1, source_target_pairs={{0,2},{1,3},{2,0},{3,1},{4,6},{5,7},{6,4},{7,5},{8,10},{9,11},{10,... | collective-permute-start | bytes 344072 | tf_op jit(solution)/shard_map/ppermute | solution.py:226

commit v5 on v4

--- a/solution.py
+++ b/solution.py
@@ -177,7 +177,7 @@
     )(near(mine), near(theirs), near(square))
 
 
-def combine_kernel(signed_ref, own_ref, other_ref, out_ref, *, sources, first, last, cap):
+def combine_kernel(signed_ref, own_ref, other_ref, *outs, sources, first, last, cap):
     me = lax.axis_index("expert")
     experts = own_ref.shape[0]
     tokens, every = signed_ref.shape[1:]
@@ -208,16 +208,16 @@
             part = jnp.concatenate([own_ref[:, source, part, :], other_ref[:, source, part, :]], axis=0)
             total = jnp.dot(left, part.reshape(depth, LANES), preferred_element_type=jnp.float32)
             total = total[:half] + total[half:]
-            out_ref[i, (b - first) * half : (b - first + 1) * half, :] = total.astype(out_ref.dtype)
+            outs[i][(b - first) * half : (b - first + 1) * half, :] = total.astype(outs[i].dtype)
 
 
 def combine(signed, own, other, sources, first, last, cap, dtype):
     rows = (last - first) * GROUP
     return pl.pallas_call(
         functools.partial(combine_kernel, sources=sources, first=first, last=last, cap=cap),
-        out_shape=pltpu.VMEM((len(sources), rows * signed.shape[1], LANES), dtype),
+        out_shape=[pltpu.VMEM((rows * signed.shape[1], LANES), dtype)] * len(sources),
         in_specs=[VMEM, VMEM, VMEM],
-        out_specs=VMEM,
+        out_specs=[VMEM] * len(sources),
         compiler_params=params(),
     )(near(signed), near(own), near(other))
 
@@ -254,14 +254,14 @@
         return combine(tiles, own, other, sources, first, last, cap, dtype)
 
     part = sums([(1, d) for d in range(low)], 0, groups, jnp.bfloat16)
-    near_sums = swap(part, 2 * low).astype(jnp.float32)
-    cut = groups // 2
-    chunks = {"c": (0, cut), "d": (cut, groups)}
+    near_sums = swap(jnp.stack(part), 2 * low).astype(jnp.float32)
     distant = list(range(2, high))
+    half = (len(distant) + 1) // 2
+    chunks = {"c": distant[:half], "d": distant[half:]}
     arrived = {}
-    for key, (first, last) in chunks.items():
-        part = sums([(h, d) for d in range(1, low) for h in distant], first, last, jnp.bfloat16)
-        part = part.reshape(low - 1, len(distant), -1, LANES)
+    for key, hs in chunks.items():
+        part = sums([(h, d) for d in range(1, low) for h in hs], 0, groups, jnp.bfloat16)
+        part = jnp.stack(part).reshape(low - 1, len(hs), -1, LANES)
         arrived[key] = [swap(part[d - 1], 2 * d) for d in range(1, low)]
     kept = sums([(0, d) for d in range(low)] + [(h, 0) for h in distant], 0, groups, jnp.float32)
     combined = kept[0] + near_sums[0]
@@ -269,15 +269,16 @@
         moved = swap((kept[d] + near_sums[d]).astype(jnp.bfloat16), 2 * d)
         combined = combined + moved.astype(jnp.float32)
 
-    def second(key, i):
-        first, last = chunks[key]
-        out = kept[low + i, first * GROUP * tokens : last * GROUP * tokens]
-        for m in arrived[key]:
-            out = out + m[i].astype(jnp.float32)
-        return swap(out.astype(jnp.bfloat16), 2 * low * distant[i]).astype(jnp.float32)
-
-    moved = {key: [second(key, i) for i in range(len(distant))] for key in chunks}
-    combined = combined + jnp.concatenate([sum(some[1:], some[0]) for some in moved.values()])
+    moved = []
+    for key, hs in chunks.items():
+        for i, h in enumerate(hs):
+            out = kept[low + distant.index(h)]
+            for m in arrived[key]:
+                out = out + m[i].astype(jnp.float32)
+            moved.append(swap(out.astype(jnp.bfloat16), 2 * low * h).astype(jnp.float32))
+
+    for m in moved:
+        combined = combined + m
     combined = combined.astype(jnp.bfloat16).reshape(tiles, tokens, LANES)
     combined = combined.transpose(1, 0, 2).reshape(tokens, width)
 

time: 42 us -> 39.7 us (0.945)
  starting transfers between devices: 18.5 us -> 15.4 us
  waiting for transfers between devices: 14.7 us -> 15.6 us
    ppermute x15 -> x13, starting transfers between devices: 18.5 us -> 15.4 us  [exchange(): return lax.ppermute(x, axis, [(i, i ^ bit) for i in range(size)])]
    ppermute x15 -> x13, waiting for transfers between devices: 14.7 us -> 15.6 us  [exchange(): return lax.ppermute(x, axis, [(i, i ^ bit) for i in range(size)])]
  transfers between devices with their start and end apart: 15 -> 13, of which waited for: 7 -> 8; matrix products, arithmetic and copies ran while one was open for 2% -> 2% of each run, Pallas kernels for 14% -> 15%
where the time goes in v5:
time: 39.7 us; the launch traced here: 39.5 us
  waiting for transfers between devices  15.6 us (39%)
  starting transfers between devices  15.4 us (39%)
  Pallas kernels  6.34 us (16%)
  other arithmetic  1.4 us (4%)
  between operations  0.76 us (2%)
    ppermute x13, waiting for transfers between devices, exchange(): return lax.ppermute(x, axis, [(i, i ^ bit) for i in range(size)])  15.6 us
    ppermute x13, starting transfers between devices, exchange(): return lax.ppermute(x, axis, [(i, i ^ bit) for i in range(size)])  15.4 us
    pallas_call x4, Pallas kernels, combine(): pl.pallas_call(functools.partial(combine_kernel, sources=sources, first=f...  2.1 us
    pallas_call x1, Pallas kernels, load(): pl.pallas_call(load_kernel, out_shape=pltpu.VMEM(own.shape, own.dtype), i...  2.05 us
    pallas_call x1, Pallas kernels, squares(): pl.pallas_call(squares_kernel, out_shape=pltpu.VMEM((experts, 8, holders...  0.88 us
    pallas_call x1, Pallas kernels, weights(): pl.pallas_call(weights_kernel, out_shape=pltpu.VMEM((ids.shape[0], expert...  0.81 us
  transfers between devices with their start and end apart: 13, of which 8 were waited for; matrix products, arithmetic and copies ran while one was open for 2% of the time, Pallas kernels for 15%

profile of v5, /device:TPU:0, one launch (start us, length us, event | category | flops | bytes accessed | tf_op | source)
XLA Modules:
  0.0 39.5 jit_solution(16342840365994821307)
XLA Ops:
  0.6 0.6 %collective-permute-start.3 = (bf16[8,16,112,128]{3,2,1,0:T(8,128)(2,1)}, bf16[8,16,112,128]{3,2,1,0:T(8,128)(2,1)S(1)}, u32[]{:S(2)}, u32[]{:S(2)}) collective-permute-start(bf16[8,16,112,128]{3,2,1,0:T(8,128)(2,1)} %bitcast.55), channel_id=1, source_target_pairs={{0,1},{1,0},{2,3},{3,2},{4,5},{5,4},{6,7},{7,6},{8,9},{9,8},{10,11... | collective-permute-start | bytes 11010056 | tf_op jit(solution)/shard_map/ppermute | solution.py:226
  1.2 0.8 %weights.1 = f32[8,128]{1,0:T(8,128)S(1)} custom-call(s32[8,8]{1,0:T(8,128)} %ids_hbm.1, f32[8,8]{1,0:T(8,128)} %gates_hbm.1), custom_call_target="tpu_custom_call" | custom-call | tf_op jit(solution)/shard_map/weights/pallas_call | solution.py:69
  2.0 2.6 %collective-permute-start = (f32[8,128]{1,0:T(8,128)S(1)}, f32[8,128]{1,0:T(8,128)S(1)}, u32[]{:S(2)}, u32[]{:S(2)}) collective-permute-start(f32[8,128]{1,0:T(8,128)S(1)} %weights.1), channel_id=1, source_target_pairs={{0,2},{1,3},{2,0},{3,1},{4,6},{5,7},{6,4},{7,5},{8,10},{9,11},{10,... | collective-permute-start | bytes 12296 | tf_op jit(solution)/shard_map/ppermute | solution.py:226
  4.6 2.0 %load.1.own_ref = bf16[8,16,112,128]{3,2,1,0:T(8,128)(2,1)S(1)} custom-call(bf16[8,16,112,128]{3,2,1,0:T(8,128)(2,1)} %bitcast.56), custom_call_target="tpu_custom_call" | custom-call | tf_op jit(solution)/shard_map/load/pallas_call | solution.py:91
  6.7 0.9 %squares.1.squares_ref = f32[8,8,128]{2,1,0:T(8,128)S(1)} custom-call(bf16[8,16,112,128]{3,2,1,0:T(8,128)(2,1)S(1)} %load.1.own_ref), custom_call_target="tpu_custom_call" | custom-call | tf_op jit(solution)/shard_map/squares/pallas_call | solution.py:124
  7.6 3.7 %collective-permute-start.2 = (f32[2,8,128]{2,1,0:T(8,128)S(1)}, f32[2,8,128]{2,1,0:T(8,128)S(1)}, u32[]{:S(2)}, u32[]{:S(2)}) collective-permute-start(f32[2,8,128]{2,1,0:T(8,128)S(1)} %pad_maximum_fusion.2), channel_id=1, source_target_pairs={{0,12},{1,13},{2,14},{3,15},{4,8},{5,9},{6,10},{7,11},{8,4},{9,5},... | collective-permute-start | bytes 24584 | tf_op jit(solution)/shard_map/ppermute | solution.py:226
  11.2 0.8 %collective-permute-start.4 = (f32[2,8,128]{2,1,0:T(8,128)S(1)}, f32[2,8,128]{2,1,0:T(8,128)S(1)}, u32[]{:S(2)}, u32[]{:S(2)}) collective-permute-start(f32[2,8,128]{2,1,0:T(8,128)S(1)} %pad_maximum_fusion.2), channel_id=1, source_target_pairs={{0,4},{1,5},{2,6},{3,7},{4,0},{5,1},{6,2},{7,3},{8,12},{9,13},{10,... | collective-permute-start | bytes 24584 | tf_op jit(solution)/shard_map/ppermute | solution.py:226
  12.0 2.9 %collective-permute-done.4.signed_ref = f32[2,8,128]{2,1,0:T(8,128)S(1)} collective-permute-done((f32[2,8,128]{2,1,0:T(8,128)S(1)}, f32[2,8,128]{2,1,0:T(8,128)S(1)}, u32[]{:S(2)}, u32[]{:S(2)}) %collective-permute-start.4) | collective-permute-done | bytes 8224 | tf_op jit(solution)/shard_map/ppermute | solution.py:226
  14.9 0.9 %collective-permute-done.1 = f32[2,8,128]{2,1,0:T(8,128)S(1)} collective-permute-done((f32[2,8,128]{2,1,0:T(8,128)S(1)}, f32[2,8,128]{2,1,0:T(8,128)S(1)}, u32[]{:S(2)}, u32[]{:S(2)}) %collective-permute-start.1) | collective-permute-done | bytes 8224 | tf_op jit(solution)/shard_map/ppermute | solution.py:226
  15.9 1.2 %collective-permute-done.11.theirs_ref = f32[8,8,128]{2,1,0:T(8,128)S(1)} collective-permute-done((f32[8,8,128]{2,1,0:T(8,128)S(1)}, f32[8,8,128]{2,1,0:T(8,128)S(1)}, u32[]{:S(2)}, u32[]{:S(2)}) %collective-permute-start.11) | collective-permute-done | bytes 32800 | tf_op jit(solution)/shard_map/ppermute | solution.py:226
  17.5 1.5 %collective-permute-start.12 = (f32[8,8]{1,0:T(8,128)S(1)}, f32[8,8]{1,0:T(8,128)S(1)}, u32[]{:S(2)}, u32[]{:S(2)}) collective-permute-start(f32[8,8]{1,0:T(8,128)S(1)} %statistics.1), channel_id=1, source_target_pairs={{0,16},{16,0},{1,17},{17,1},{2,18},{18,2},{3,19},{19,3},{4,20},{20... | collective-permute-start | bytes 776 | tf_op jit(solution)/shard_map/ppermute | solution.py:226
  19.1 2.1 %collective-permute-done.12 = f32[8,8]{1,0:T(8,128)S(1)} collective-permute-done((f32[8,8]{1,0:T(8,128)S(1)}, f32[8,8]{1,0:T(8,128)S(1)}, u32[]{:S(2)}, u32[]{:S(2)}) %collective-permute-start.12) | collective-permute-done | bytes 288 | tf_op jit(solution)/shard_map/ppermute | solution.py:226
  21.6 0.7 %collective-permute-start.9 = (bf16[1,448,128]{2,1,0:T(8,128)(2,1)S(1)}, bf16[1,448,128]{2,1,0:T(8,128)(2,1)S(1)}, u32[]{:S(2)}, u32[]{:S(2)}) collective-permute-start(bf16[1,448,128]{2,1,0:T(8,128)(2,1)S(1)} %bitcast.50), channel_id=1, source_target_pairs={{0,2},{1,3},{2,0},{3,1},{4,6},{5,7},{6,4},{7,5},{8,10},{9,11},{10,... | collective-permute-start | bytes 344072 | tf_op jit(solution)/shard_map/ppermute | solution.py:226
  22.7 1.5 %collective-permute-start.7 = (bf16[1,448,128]{2,1,0:T(8,128)(2,1)S(1)}, bf16[1,448,128]{2,1,0:T(8,128)(2,1)S(1)}, u32[]{:S(2)}, u32[]{:S(2)}) collective-permute-start(bf16[1,448,128]{2,1,0:T(8,128)(2,1)S(1)} %bitcast.49), channel_id=1, source_target_pairs={{0,2},{1,3},{2,0},{3,1},{4,6},{5,7},{6,4},{7,5},{8,10},{9,11},{10,... | collective-permute-start | bytes 344072 | tf_op jit(solution)/shard_map/ppermute | solution.py:226
  24.8 0.8 %shard_map.58 = (f32[448,128]{1,0:T(8,128)S(1)}, f32[448,128]{1,0:T(8,128)S(1)}, f32[448,128]{1,0:T(8,128)S(1)}, f32[448,128]{1,0:T(8,128)S(1)}) custom-call(f32[4,8,128]{2,1,0:T(8,128)S(1)} %pad_maximum_fusion.1.signed_ref, bf16[8,16,112,128]{3,2,1,0:T(8,128)(2,1)S(1)} %load.1.own_ref, bf16[8,16,112,128]{3,2,1,0:T(8,128)(2,1)S(1)} %collective-permute-done.3.other_ref), custom_call_target="tpu_custom_call" | custom-call | tf_op jit(solution)/shard_map/pallas_call | solution.py:216
  25.6 1.4 %collective-permute-done.9 = bf16[1,448,128]{2,1,0:T(8,128)(2,1)S(1)} collective-permute-done((bf16[1,448,128]{2,1,0:T(8,128)(2,1)S(1)}, bf16[1,448,128]{2,1,0:T(8,128)(2,1)S(1)}, u32[]{:S(2)}, u32[]{:S(2)}) %collective-permute-start.9) | collective-permute-done | bytes 114720 | tf_op jit(solution)/shard_map/ppermute | solution.py:226
  27.0 2.2 %collective-permute-start.10 = (bf16[448,128]{1,0:T(8,128)(2,1)S(1)}, bf16[448,128]{1,0:T(8,128)(2,1)S(1)}, u32[]{:S(2)}, u32[]{:S(2)}) collective-permute-start(bf16[448,128]{1,0:T(8,128)(2,1)S(1)} %fusion.7), channel_id=1, source_target_pairs={{0,12},{1,13},{2,14},{3,15},{4,8},{5,9},{6,10},{7,11},{8,4},{9,5},... | collective-permute-start | bytes 344072 | tf_op jit(solution)/shard_map/ppermute | solution.py:226
  29.2 1.1 %collective-permute-start.8 = (bf16[448,128]{1,0:T(8,128)(2,1)S(1)}, bf16[448,128]{1,0:T(8,128)(2,1)S(1)}, u32[]{:S(2)}, u32[]{:S(2)}) collective-permute-start(bf16[448,128]{1,0:T(8,128)(2,1)S(1)} %fusion.8), channel_id=1, source_target_pairs={{0,8},{1,9},{2,10},{3,11},{4,12},{5,13},{6,14},{7,15},{8,0},{9,1},... | collective-permute-start | bytes 344072 | tf_op jit(solution)/shard_map/ppermute | solution.py:226
  30.3 2.2 %collective-permute-done.5 = bf16[2,448,128]{2,1,0:T(8,128)(2,1)S(1)} collective-permute-done((bf16[2,448,128]{2,1,0:T(8,128)(2,1)S(1)}, bf16[2,448,128]{2,1,0:T(8,128)(2,1)S(1)}, u32[]{:S(2)}, u32[]{:S(2)}) %collective-permute-start.5) | collective-permute-done | bytes 229408 | tf_op jit(solution)/shard_map/ppermute | solution.py:226
  32.6 0.7 %collective-permute-start.6 = (bf16[448,128]{1,0:T(8,128)(2,1)S(1)}, bf16[448,128]{1,0:T(8,128)(2,1)S(1)}, u32[]{:S(2)}, u32[]{:S(2)}) collective-permute-start(bf16[448,128]{1,0:T(8,128)(2,1)S(1)} %fusion.1), channel_id=1, source_target_pairs={{0,2},{1,3},{2,0},{3,1},{4,6},{5,7},{6,4},{7,5},{8,10},{9,11},{10,... | collective-permute-start | bytes 344072 | tf_op jit(solution)/shard_map/ppermute | solution.py:226
  33.3 0.5 %sqrt_bitcast_fusion = (f32[8]{0:T(128)}, s32[8]{0:T(128)}) fusion(f32[8,8]{1,0:T(8,128)S(1)} %add.35), kind=kLoop, calls=%fused_computation.22 | loop fusion | flops 32 | bytes 128 | tf_op jit(solution)/shard_map/sqrt | solution.py:295
  33.8 2.2 %collective-permute-done.10 = bf16[448,128]{1,0:T(8,128)(2,1)S(1)} collective-permute-done((bf16[448,128]{1,0:T(8,128)(2,1)S(1)}, bf16[448,128]{1,0:T(8,128)(2,1)S(1)}, u32[]{:S(2)}, u32[]{:S(2)}) %collective-permute-start.10) | collective-permute-done | bytes 114720 | tf_op jit(solution)/shard_map/ppermute | solution.py:226
  36.0 2.8 %collective-permute-done.8 = bf16[448,128]{1,0:T(8,128)(2,1)S(1)} collective-permute-done((bf16[448,128]{1,0:T(8,128)(2,1)S(1)}, bf16[448,128]{1,0:T(8,128)(2,1)S(1)}, u32[]{:S(2)}, u32[]{:S(2)}) %collective-permute-start.8) | collective-permute-done | bytes 114720 | tf_op jit(solution)/shard_map/ppermute | solution.py:226
  38.8 0.7 %fusion.9 = bf16[8,7168]{1,0:T(8,128)(2,1)} fusion(bf16[448,128]{1,0:T(8,128)(2,1)S(1)} %collective-permute-done.10, bf16[448,128]{1,0:T(8,128)(2,1)S(1)} %collective-permute-done.8, bf16[448,128]{1,0:T(8,128)(2,1)S(1)} %collective-permute-done.6, f32[448,128]{1,0:T(8,128)S(1)} %get-tuple-element.9, f32[2,448,128]{2,1,0:T(8,128)S(1)} %convert_element_type.42), kind=kLoop, calls=%fused_computation.14 | loop fusion | flops 458752 | bytes 917504 | tf_op jit(solution)/shard_map/reshape | solution.py:283
  (27 shorter events, 2.2 us)
Async XLA Ops:
  0.6 20.6 %collective-permute-start.3 = (bf16[8,16,112,128]{3,2,1,0:T(8,128)(2,1)}, bf16[8,16,112,128]{3,2,1,0:T(8,128)(2,1)S(1)}, u32[]{:S(2)}, u32[]{:S(2)}) collective-permute-start(bf16[8,16,112,128]{3,2,1,0:T(8,128)(2,1)} %bitcast.55), channel_id=1, source_target_pairs={{0,1},{1,0},{2,3},{3,2},{4,5},{5,4},{6,7},{7,6},{8,9},{9,8},{10,11... | collective-permute-start | bytes 11010056 | tf_op jit(solution)/shard_map/ppermute | solution.py:226
  2.0 5.5 %collective-permute-start = (f32[8,128]{1,0:T(8,128)S(1)}, f32[8,128]{1,0:T(8,128)S(1)}, u32[]{:S(2)}, u32[]{:S(2)}) collective-permute-start(f32[8,128]{1,0:T(8,128)S(1)} %weights.1), channel_id=1, source_target_pairs={{0,2},{1,3},{2,0},{3,1},{4,6},{5,7},{6,4},{7,5},{8,10},{9,11},{10,... | collective-permute-start | bytes 12296 | tf_op jit(solution)/shard_map/ppermute | solution.py:226
  7.6 8.2 %collective-permute-start.2 = (f32[2,8,128]{2,1,0:T(8,128)S(1)}, f32[2,8,128]{2,1,0:T(8,128)S(1)}, u32[]{:S(2)}, u32[]{:S(2)}) collective-permute-start(f32[2,8,128]{2,1,0:T(8,128)S(1)} %pad_maximum_fusion.2), channel_id=1, source_target_pairs={{0,12},{1,13},{2,14},{3,15},{4,8},{5,9},{6,10},{7,11},{8,4},{9,5},... | collective-permute-start | bytes 24584 | tf_op jit(solution)/shard_map/ppermute | solution.py:226
  11.2 4.5 %collective-permute-start.1 = (f32[2,8,128]{2,1,0:T(8,128)S(1)}, f32[2,8,128]{2,1,0:T(8,128)S(1)}, u32[]{:S(2)}, u32[]{:S(2)}) collective-permute-start(f32[2,8,128]{2,1,0:T(8,128)S(1)} %pad_maximum_fusion.2), channel_id=1, source_target_pairs={{0,8},{1,9},{2,10},{3,11},{4,12},{5,13},{6,14},{7,15},{8,0},{9,1},... | collective-permute-start | bytes 24584 | tf_op jit(solution)/shard_map/ppermute | solution.py:226
  11.2 3.7 %collective-permute-start.4 = (f32[2,8,128]{2,1,0:T(8,128)S(1)}, f32[2,8,128]{2,1,0:T(8,128)S(1)}, u32[]{:S(2)}, u32[]{:S(2)}) collective-permute-start(f32[2,8,128]{2,1,0:T(8,128)S(1)} %pad_maximum_fusion.2), channel_id=1, source_target_pairs={{0,4},{1,5},{2,6},{3,7},{4,0},{5,1},{6,2},{7,3},{8,12},{9,13},{10,... | collective-permute-start | bytes 24584 | tf_op jit(solution)/shard_map/ppermute | solution.py:226
  15.8 1.3 %collective-permute-start.11 = (f32[8,8,128]{2,1,0:T(8,128)S(1)}, f32[8,8,128]{2,1,0:T(8,128)S(1)}, u32[]{:S(2)}, u32[]{:S(2)}) collective-permute-start(f32[8,8,128]{2,1,0:T(8,128)S(1)} %constant_dynamic-update-slice_fusion.mine_ref), channel_id=1, source_target_pairs={{0,1},{1,0},{2,3},{3,2},{4,5},{5,4},{6,7},{7,6},{8,9},{9,8},{10,11... | collective-permute-start | bytes 98312 | tf_op jit(solution)/shard_map/ppermute | solution.py:226
  17.5 3.6 %collective-permute-start.12 = (f32[8,8]{1,0:T(8,128)S(1)}, f32[8,8]{1,0:T(8,128)S(1)}, u32[]{:S(2)}, u32[]{:S(2)}) collective-permute-start(f32[8,8]{1,0:T(8,128)S(1)} %statistics.1), channel_id=1, source_target_pairs={{0,16},{16,0},{1,17},{17,1},{2,18},{18,2},{3,19},{19,3},{4,20},{20... | collective-permute-start | bytes 776 | tf_op jit(solution)/shard_map/ppermute | solution.py:226
  21.6 5.4 %collective-permute-start.9 = (bf16[1,448,128]{2,1,0:T(8,128)(2,1)S(1)}, bf16[1,448,128]{2,1,0:T(8,128)(2,1)S(1)}, u32[]{:S(2)}, u32[]{:S(2)}) collective-permute-start(bf16[1,448,128]{2,1,0:T(8,128)(2,1)S(1)} %bitcast.50), channel_id=1, source_target_pairs={{0,2},{1,3},{2,0},{3,1},{4,6},{5,7},{6,4},{7,5},{8,10},{9,11},{10,... | collective-permute-start | bytes 344072 | tf_op jit(solution)/shard_map/ppermute | solution.py:226
  22.7 6.5 %collective-permute-start.7 = (bf16[1,448,128]{2,1,0:T(8,128)(2,1)S(1)}, bf16[1,448,128]{2,1,0:T(8,128)(2,1)S(1)}, u32[]{:S(2)}, u32[]{:S(2)}) collective-permute-start(bf16[1,448,128]{2,1,0:T(8,128)(2,1)S(1)} %bitcast.49), channel_id=1, source_target_pairs={{0,2},{1,3},{2,0},{3,1},{4,6},{5,7},{6,4},{7,5},{8,10},{9,11},{10,... | collective-permute-start | bytes 344072 | tf_op jit(solution)/shard_map/ppermute | solution.py:226
  24.7 7.8 %collective-permute-start.5 = (bf16[2,448,128]{2,1,0:T(8,128)(2,1)S(1)}, bf16[2,448,128]{2,1,0:T(8,128)(2,1)S(1)}, u32[]{:S(2)}, u32[]{:S(2)}) collective-permute-start(bf16[2,448,128]{2,1,0:T(8,128)(2,1)S(1)} %pad_maximum_fusion), channel_id=1, source_target_pairs={{0,4},{1,5},{2,6},{3,7},{4,0},{5,1},{6,2},{7,3},{8,12},{9,13},{10,... | collective-permute-start | bytes 688136 | tf_op jit(solution)/shard_map/ppermute | solution.py:226
  27.0 9.0 %collective-permute-start.10 = (bf16[448,128]{1,0:T(8,128)(2,1)S(1)}, bf16[448,128]{1,0:T(8,128)(2,1)S(1)}, u32[]{:S(2)}, u32[]{:S(2)}) collective-permute-start(bf16[448,128]{1,0:T(8,128)(2,1)S(1)} %fusion.7), channel_id=1, source_target_pairs={{0,12},{1,13},{2,14},{3,15},{4,8},{5,9},{6,10},{7,11},{8,4},{9,5},... | collective-permute-start | bytes 344072 | tf_op jit(solution)/shard_map/ppermute | solution.py:226
  29.2 9.6 %collective-permute-start.8 = (bf16[448,128]{1,0:T(8,128)(2,1)S(1)}, bf16[448,128]{1,0:T(8,128)(2,1)S(1)}, u32[]{:S(2)}, u32[]{:S(2)}) collective-permute-start(bf16[448,128]{1,0:T(8,128)(2,1)S(1)} %fusion.8), channel_id=1, source_target_pairs={{0,8},{1,9},{2,10},{3,11},{4,12},{5,13},{6,14},{7,15},{8,0},{9,1},... | collective-permute-start | bytes 344072 | tf_op jit(solution)/shard_map/ppermute | solution.py:226
  32.6 6.2 %collective-permute-start.6 = (bf16[448,128]{1,0:T(8,128)(2,1)S(1)}, bf16[448,128]{1,0:T(8,128)(2,1)S(1)}, u32[]{:S(2)}, u32[]{:S(2)}) collective-permute-start(bf16[448,128]{1,0:T(8,128)(2,1)S(1)} %fusion.1), channel_id=1, source_target_pairs={{0,2},{1,3},{2,0},{3,1},{4,6},{5,7},{6,4},{7,5},{8,10},{9,11},{10,... | collective-permute-start | bytes 344072 | tf_op jit(solution)/shard_map/ppermute | solution.py:226
